TPU v7x, 512 devices: a whole 4x4x16 slice. The times are simulated.
512 devices in a mesh: fsdp: 2 (over core), ctx: 64 (over y, z), dp: 4 (over x).
Axes of the slice: x: 4, y: 4, z: 16, core: 2. Of those that a mesh axis runs over, the one named last changes fastest.
Arguments:
- query_stream: bfloat16 [1, 8192, 8192], P(None, 'ctx', ('fsdp', 'dp')), may hold values from -6 to 6
- key_stream: bfloat16 [1, 8192, 8192], P(None, 'ctx', ('fsdp', 'dp')), may hold values from -6 to 6
- value_stream: bfloat16 [1, 8192, 8192], P(None, 'ctx', ('fsdp', 'dp')), may hold values from -6 to 6
- document_starts: int32 [1, 8192], replicated, may hold values 0 or 1
- medium_taps: bfloat16 [512, 128], P(None, 'fsdp'), may hold values from -0.5 to 0.5
- modal_rate: bfloat16 [512, 16], P('fsdp', 'dp'), may hold values from 2.4288893e-06 to 0.032958984
- modal_residue: bfloat16 [512, 16], P('fsdp', 'dp'), may hold values from -4 to 4
- skip_gain: float32 [8192], P(('fsdp', 'dp')), may hold values from 0.5 to 1.5
Outputs:
- hyena_out: bfloat16 [1, 8192, 8192], P(None, 'ctx', ('fsdp', 'dp'))
All inputs are finite; a program needn't handle non-finite values.
Results may differ from a plain program's by a relative error of at most 0.0085.
Values may be sent and summed in bfloat16 or wider, within the bound.
A program may use at most 64 MiB of HBM per device.

v0:
```python
import jax
import jax.numpy as jnp
from jax import lax
from jax.sharding import PartitionSpec as P

GROUP_CH = 16


highest = lax.Precision.HIGHEST


def entering_2(array, axis, combine, identity):
    count, position = (lax.axis_size(axis), lax.axis_index(axis))
    everything = jax.tree.map(lambda part: lax.all_gather(part, axis), array)
    start = jax.tree.map(
        lambda part, zero: jnp.broadcast_to(jnp.asarray(zero, part.dtype), part.shape),
        array,
        identity,
    )

    def turn(k, before):
        reached = k < position
        new = combine(before, jax.tree.map(lambda part: part[k], everything))
        return jax.tree.map(lambda a, b: jnp.where(reached, a, b), new, before)

    return lax.fori_loop(0, count, turn, start)


def toeplitz_taps(filters, block_len):
    groups = filters.shape[0]
    line = jnp.concatenate(
        [
            jnp.zeros((groups, 1), filters.dtype),
            filters[:, ::-1],
            jnp.zeros((groups, block_len), filters.dtype),
        ],
        axis=1,
    )
    tiled = jnp.tile(line, (1, block_len))[:, : 2 * block_len * block_len]
    return tiled.reshape(groups, block_len, 2 * block_len)


def medium_conv(extended, padded_docs, filters):
    block_len = filters.shape[1]
    groups = filters.shape[0]
    channels = extended.shape[2]
    row_count = extended.shape[0] - block_len
    block_count = row_count // block_len
    matrix = toeplitz_taps(filters, block_len)
    previous = extended[:row_count].reshape(block_count, block_len, groups, channels)
    current = extended[block_len:].reshape(block_count, block_len, groups, channels)
    windows = jnp.concatenate([previous, current], axis=1)
    row_docs = padded_docs[block_len:].reshape(block_count, block_len)
    window_docs = jnp.concatenate(
        [padded_docs[:row_count].reshape(block_count, block_len), row_docs], axis=1
    )
    doc_masks = row_docs[:, :, None] == window_docs[:, None, :]
    nothing = jnp.zeros((), matrix.dtype)

    def apply_part(inputs):
        mask_part, window_part = inputs
        masked = jnp.where(mask_part[:, None], matrix[None], nothing)
        return jnp.einsum(
            "ngtj,njgc->ntgc", masked, window_part, preferred_element_type=jnp.float32
        )

    outputs = lax.map(
        apply_part,
        (
            doc_masks.reshape(16, block_count // 16, block_len, 2 * block_len),
            windows.reshape(16, block_count // 16, 2 * block_len, groups, channels),
        ),
    )
    return outputs.reshape(row_count, groups, channels)


def modal_blocks(values, doc_index, starts, decay_rate, scaled, carry_state, block_len):
    row_count = values.shape[0]
    block_count = row_count // block_len
    groups = values.shape[1]
    channels = values.shape[2]
    lag_steps = jnp.arange(block_len + 1, dtype=jnp.float32)
    powers = jnp.exp(-decay_rate[:, :, None] * lag_steps)
    kernel = jnp.einsum("gn,gnk->gk", scaled, powers[:, :, :block_len], precision=highest)
    positions = jnp.arange(block_len, dtype=jnp.int32)
    offsets = positions[:, None] - positions[None, :]
    causal = offsets >= 0
    toeplitz = toeplitz_taps(kernel, block_len)[:, :, block_len:]
    carry_weight = scaled[:, None, :] * jnp.transpose(powers[:, :, 1:], (0, 2, 1))
    end_weight = powers[:, :, :block_len][:, :, ::-1]
    full_decay = jnp.transpose(powers[:, :, block_len])

    def advance(state_now, inputs):
        block_values, block_docs, block_starts = inputs
        before = block_docs[0] - block_starts[0]
        continues = block_docs == before
        same_doc = causal & (block_docs[:, None] == block_docs[None, :])
        local_part = jnp.einsum(
            "gts,sgc->tgc",
            jnp.where(same_doc[None], toeplitz, 0.0),
            block_values,
            precision=highest,
        )
        carried = jnp.einsum(
            "gtn,ngc->tgc",
            jnp.where(continues[None, :, None], carry_weight, 0.0),
            state_now,
            precision=highest,
        )
        keep_mask = block_docs == block_docs[block_len - 1]
        emitted = jnp.einsum(
            "gns,sgc->ngc",
            jnp.where(keep_mask[None, None, :], end_weight, 0.0),
            block_values,
            precision=highest,
        )
        factor = jnp.where(continues[block_len - 1], full_decay, 0.0)
        return (factor[:, :, None] * state_now + emitted, local_part + carried)

    final_state, outputs = lax.scan(
        advance,
        carry_state,
        (
            values.reshape(block_count, block_len, groups, channels),
            doc_index.reshape(block_count, block_len),
            starts.reshape(block_count, block_len),
        ),
    )
    return (outputs.reshape(row_count, groups, channels), final_state)


def merge_carry(earlier, latter):
    decay_first, state_first = earlier
    decay_second, state_second = latter
    spread = state_first.reshape(decay_first.shape[0], decay_first.shape[1], -1)
    moved = (decay_second[:, :, None] * spread).reshape(state_first.shape)
    return (decay_first * decay_second, moved + state_second)


def body(
    query_stream,
    key_stream,
    value_stream,
    document_starts,
    medium_taps,
    modal_rate,
    modal_residue,
    skip_gain,
):
    tokens = query_stream.shape[1]
    local_width = query_stream.shape[2]
    fsdp_size = lax.axis_size("fsdp")
    dp_size = lax.axis_size("dp")
    dp_place = lax.axis_index("dp")
    block_len = medium_taps.shape[1] * fsdp_size
    ctx_size = lax.axis_size("ctx")
    ctx_place = lax.axis_index("ctx")
    groups_here = local_width // GROUP_CH
    product = (key_stream[0].astype(jnp.float32) * value_stream[0].astype(jnp.float32)).astype(
        jnp.bfloat16
    )
    starts = document_starts[0]
    doc_index = jnp.cumsum(starts)
    padded_docs = jnp.concatenate([jnp.full((block_len,), -1, jnp.int32), doc_index])
    quarters = medium_taps.reshape(fsdp_size, dp_size, groups_here, medium_taps.shape[1])
    halves = lax.dynamic_slice_in_dim(quarters, dp_place, 1, 1)[:, 0]
    channels = local_width // ctx_size
    per_device = channels // GROUP_CH
    own_rows = lax.dynamic_slice_in_dim(halves, ctx_place * per_device, per_device, 1)
    filters = lax.all_to_all(own_rows, "fsdp", split_axis=0, concat_axis=2, tiled=True)[0]
    outgoing = (
        product.reshape(tokens, ctx_size, channels)
        .transpose(1, 0, 2)
        .reshape(ctx_size, tokens * channels)
    )
    incoming = lax.all_to_all(outgoing, "ctx", split_axis=0, concat_axis=0, tiled=True)
    sequence = incoming.reshape(ctx_size * tokens, channels)
    extended = jnp.concatenate([jnp.zeros((block_len, channels), jnp.bfloat16), sequence]).reshape(
        -1, per_device, GROUP_CH
    )
    medium = medium_conv(extended, padded_docs, filters).astype(jnp.bfloat16)
    returned = lax.all_to_all(
        medium.reshape(ctx_size, tokens * channels), "ctx", split_axis=0, concat_axis=0, tiled=True
    )
    medium_local = (
        returned.reshape(ctx_size, tokens, channels).transpose(1, 0, 2).reshape(tokens, local_width)
    )
    gated_values = (query_stream[0].astype(jnp.float32) * medium_local.astype(jnp.float32)).astype(
        jnp.bfloat16
    )
    rate_all, residue_all = (
        lax.all_to_all(modal_rate, "dp", split_axis=0, concat_axis=1, tiled=True),
        lax.all_to_all(modal_residue, "dp", split_axis=0, concat_axis=1, tiled=True),
    )
    decay_rate = rate_all.astype(jnp.float32)
    mode_count = decay_rate.shape[1]
    scaled = residue_all.astype(jnp.float32) * jnp.sqrt(
        (1.0 - jnp.exp(-2.0 * decay_rate)) / mode_count
    )
    local_docs = lax.dynamic_slice_in_dim(doc_index, ctx_place * tokens, tokens, 0)
    local_starts = lax.dynamic_slice_in_dim(starts, ctx_place * tokens, tokens, 0)
    values = gated_values.astype(jnp.float32).reshape(tokens, groups_here, GROUP_CH)
    part_count = 4
    part_groups = groups_here // part_count
    split_values = values.reshape(tokens, part_count, part_groups, GROUP_CH).transpose(1, 0, 2, 3)

    def run_part(inputs):
        part_values, part_rate, part_scaled = inputs
        zero_state = jnp.zeros((mode_count, part_groups, GROUP_CH), jnp.float32)
        return modal_blocks(
            part_values, local_docs, local_starts, part_rate, part_scaled, zero_state, block_len
        )

    local_parts, end_parts = lax.map(
        run_part,
        (
            split_values,
            decay_rate.reshape(part_count, part_groups, mode_count),
            scaled.reshape(part_count, part_groups, mode_count),
        ),
    )
    local_long = local_parts.transpose(1, 0, 2, 3).reshape(tokens, local_width)
    end_states = end_parts.transpose(1, 0, 2, 3).reshape(mode_count, local_width)
    continues = local_docs == local_docs[0] - local_starts[0]
    factor = jnp.where(continues[tokens - 1], jnp.transpose(jnp.exp(-decay_rate * tokens)), 0.0)
    prefix_decay, entering = entering_2(
        (factor, end_states),
        "ctx",
        merge_carry,
        (jnp.ones_like(factor), jnp.zeros_like(end_states)),
    )
    lag_steps = jnp.arange(1, tokens + 1, dtype=jnp.float32)
    weights = scaled[:, :, None] * jnp.exp(-decay_rate[:, :, None] * lag_steps)
    masked = jnp.where(continues[None, None, :], weights, 0.0)
    carried = jnp.einsum(
        "gnt,ngc->tgc",
        masked,
        entering.reshape(mode_count, groups_here, GROUP_CH),
        precision=highest,
    )
    combined = (
        local_long
        + carried.reshape(tokens, local_width)
        + skip_gain[None, :] * gated_values.astype(jnp.float32)
    )
    return combined.astype(jnp.bfloat16)[None]


def solution(mesh):
    return jax.shard_map(
        body,
        mesh=mesh,
        in_specs=(
            P(None, "ctx", ("fsdp", "dp")),
            P(None, "ctx", ("fsdp", "dp")),
            P(None, "ctx", ("fsdp", "dp")),
            P(),
            P(None, "fsdp"),
            P("fsdp", "dp"),
            P("fsdp", "dp"),
            P(("fsdp", "dp")),
        ),
        out_specs=P(None, "ctx", ("fsdp", "dp")),
        check_vma=False,
    )
```

profile of v0, /device:TPU:24, one launch (start us, length us, event | category | flops | bytes accessed | tf_op | source)
XLA Modules:
  0.0 444.7 jit_solution(15580213425937911821)
XLA Ops:
  8.3 3.2 all-to-all-start.1
  12.9 1.1 copy.100
  14.0 1.1 copy.101
  18.6 18.7 %all-to-all-start = ((bf16[64,2,1024]{2,1,0:T(2,128)(2,1)}), bf16[64,2,1024]{2,1,0:T(2,128)(2,1)S(1)}, u32[]{:S(2)}, u32[]{:S(2)}) async-start(bf16[64,2,1024]{2,1,0:T(2,128)(2,1)} %reshape.388), calls=%async_computation | async-start | bytes 524288 | tf_op jit(solution)/shard_map/all_to_all | solution.py:176
  39.9 2.7 broadcast_compare_fusion.2
  42.5 16.2 %all-to-all-done = bf16[64,2,1024]{2,1,0:T(2,128)(2,1)S(1)} async-done(((bf16[64,2,1024]{2,1,0:T(2,128)(2,1)}), bf16[64,2,1024]{2,1,0:T(2,128)(2,1)S(1)}, u32[]{:S(2)}, u32[]{:S(2)}) %all-to-all-start) | async-done | bytes 262176 | tf_op jit(solution)/shard_map/all_to_all | solution.py:176
  58.8 4.3 all-to-all-start.3
  63.3 1.5 reduce.1
  64.8 1.7 concatenate.27
  66.5 2.7 reshape.350
  70.2 2.0 pad_slice_fusion
  73.5 4.8 %all-to-all-start.4 = ((bf16[4,2,128]{2,1,0:T(2,128)(2,1)}), bf16[4,2,128]{2,1,0:T(2,128)(2,1)S(1)}, u32[]{:S(2)}, u32[]{:S(2)}) async-start(bf16[4,2,128]{2,1,0:T(2,128)(2,1)} %reshape.394), calls=%async_computation.4 | async-start | bytes 4096 | tf_op jit(solution)/shard_map/all_to_all | solution.py:192
  78.3 24.6 %while.43 = (s32[]{:T(128)}, bf16[16,4,128,1,16]{2,4,1,3,0:T(8,128)(2,1)S(1)}, bf16[16,4,256,1,16]{2,1,0,4,3:T(4,128)(2,1)S(1)}, pred[16,4,128,256]{3,2,1,0:T(32...) while((s32[]{:T(128)}, bf16[16,4,128,1,16]{2,4,1,3,0:T(8,128)(2,1)S(1)}, ...), condition=%wide.region_3.4_spmd, body=%wide.region_2.3_spmd.sunk | while | flops 4325378 | bytes 590939 | solution.py:67
  78.7 1.1 fusion.70
  80.3 1.1 fusion.70
  81.8 1.1 fusion.70
  83.3 1.1 fusion.70
  84.9 1.1 fusion.70
  86.4 1.1 fusion.70
  87.9 1.1 fusion.70
  89.5 1.1 fusion.70
  91.0 1.1 fusion.70
  92.5 1.1 fusion.70
  94.1 1.1 fusion.70
  95.6 1.1 fusion.70
  97.2 1.1 fusion.70
  98.7 1.1 fusion.70
  101.8 1.1 fusion.70
  103.9 1.5 convert_element_type.170
  105.4 2.1 reduce.10
  108.4 6.6 %all-to-all-start.2 = ((bf16[64,2,1024]{2,1,0:T(2,128)(2,1)}), bf16[64,2,1024]{2,1,0:T(2,128)(2,1)S(1)}, u32[]{:S(2)}, u32[]{:S(2)}) async-start(bf16[64,2,1024]{2,1,0:T(2,128)(2,1)} %reshape.390), calls=%async_computation.2 | async-start | bytes 524288 | tf_op jit(solution)/shard_map/all_to_all | solution.py:182
  116.4 18.0 %all-to-all-done.2 = bf16[64,2,1024]{2,1,0:T(2,128)(2,1)S(1)} async-done(((bf16[64,2,1024]{2,1,0:T(2,128)(2,1)}), bf16[64,2,1024]{2,1,0:T(2,128)(2,1)S(1)}, u32[]{:S(2)}, u32[]{:S(2)}) %all-to-all-start.2) | async-done | bytes 262176 | tf_op jit(solution)/shard_map/all_to_all | solution.py:182
  136.4 72.8 %while.44 = (s32[]{:T(128)}, f32[4,128,16,16]{1,3,2,0:T(8,128)}, f32[4,16,16,16]{1,3,2,0:T(8,128)S(1)}, f32[4,128,16,16]{1,3,2,0:T(8,128)S(1)}, s32[128]{0:T(128...) while((s32[]{:T(128)}, f32[4,128,16,16]{1,3,2,0:T(8,128)}, ...), condition=%wide.region_5.6_spmd, body=%wide.region_4.5_spmd.sunk | while | flops 63812896 | bytes 26238936 | solution.py:214
  139.5 1.2 fusion.78
  140.7 1.9 fusion.79
  142.9 1.2 fusion.84
  145.2 2.5 tile.28
  147.7 1.6 slice-done
  150.3 1.7 fusion.81
  152.0 2.6 fusion.82
  157.7 1.2 fusion.78
  158.9 1.9 fusion.79
  161.0 1.2 fusion.84
  163.4 2.5 tile.28
  165.9 1.6 slice-done
  168.5 1.7 fusion.81
  170.2 2.6 fusion.82
  175.9 1.2 fusion.78
  177.1 1.9 fusion.79
  179.2 1.2 fusion.84
  181.6 2.5 tile.28
  184.1 1.6 slice-done
  186.7 1.7 fusion.81
  188.4 2.6 fusion.82
  194.1 1.2 fusion.78
  195.3 1.9 fusion.79
  197.4 1.2 fusion.84
  199.8 2.5 tile.28
  202.3 1.6 slice-done
  204.9 1.7 fusion.81
  206.6 2.6 fusion.82
  211.5 97.8 %all-gather = f32[1024,64]{1,0:T(8,128)S(1)} all-gather(f32[16,64]{1,0:T(8,128)S(1)} %select_bitcast_fusion), channel_id=2, replica_groups=mesh['fsdp'=2,'ctx'=64,'dp'=4] {'ctx'}, dimensions={0}, use_global_device_ids=true | all-gather | bytes 266240 | tf_op jit(solution)/shard_map/all_gather | solution.py:14
  309.3 37.4 %all-gather.3.cloned.1.call-done = f32[64,16,1024]{2,1,0:T(8,128)} async-done(((f32[1,16,1024]{2,1,0:T(8,128)}), f32[64,16,1024]{2,1,0:T(8,128)}) %all-gather.3.cloned.1.call-update) | async-done | bytes 4194320 | tf_op jit(solution)/shard_map/all_gather | solution.py:14
  346.8 89.0 %while.45 = (s32[]{:T(128)}, f32[16,1024]{1,0:T(8,128)S(1)}, s32[]{:T(128)}, f32[64,16,64]{2,1,0:T(8,128)S(1)}, f32[64,16,1024]{2,1,0:T(8,128)}, /*index=5*/s32[]{:T(128)}, s32[]{:T(128)}) while((s32[]{:T(128)}, f32[16,1024]{1,0:T(8,128)S(1)}, s32[]{:T(128)}, f32[64,16,64]{2,1,0:T(8,128)S(1)}, f32[64,16,1024]{2,1,0:T(8,128)}, ...), condition=%wide.region_7.8_spmd.clone, body=%wide.region_6.7_spmd.clone.sunk | while | flops 65540 | bytes 471153 | solution.py:26
  (516 shorter events, 136.8 us)
Async XLA Ops:
  8.3 10.2 %all-to-all-start.1 = ((bf16[2,1,64]{2,1,0:T(2,128)(2,1)}), bf16[2,1,64]{2,1,0:T(2,128)(2,1)S(1)}, u32[]{:S(2)}, u32[]{:S(2)}) async-start(bf16[2,1,64]{2,1,0:T(2,128)(2,1)} %copy.107), calls=%async_computation.1 | async-start | bytes 2048 | tf_op jit(solution)/shard_map/all_to_all | solution.py:170
  15.2 22.3 %copy-start.11 = (bf16[256,4]{0,1:T(4,128)(2,1)S(1)}, bf16[256,4]{0,1:T(4,128)(2,1)}, u32[]{:S(2)}) copy-start(bf16[256,4]{0,1:T(4,128)(2,1)} %param.19) | copy-start | bytes 6148
  15.2 23.0 %copy-start.12 = (bf16[256,4]{0,1:T(4,128)(2,1)S(1)}, bf16[256,4]{0,1:T(4,128)(2,1)}, u32[]{:S(2)}) copy-start(bf16[256,4]{0,1:T(4,128)(2,1)} %param.20) | copy-start | bytes 6148
  18.6 40.2 %all-to-all-start = ((bf16[64,2,1024]{2,1,0:T(2,128)(2,1)}), bf16[64,2,1024]{2,1,0:T(2,128)(2,1)S(1)}, u32[]{:S(2)}, u32[]{:S(2)}) async-start(bf16[64,2,1024]{2,1,0:T(2,128)(2,1)} %reshape.388), calls=%async_computation | async-start | bytes 524288 | tf_op jit(solution)/shard_map/all_to_all | solution.py:176
  39.8 26.7 %copy-start.3 = (bf16[1,32896]{1,0:T(2,128)(2,1)}, bf16[1,32896]{1,0:T(2,128)(2,1)S(1)}, u32[]{:S(2)}) copy-start(bf16[1,32896]{1,0:T(2,128)(2,1)S(1)} %tile.24) | copy-start | bytes 197380
  58.8 14.7 %all-to-all-start.3 = ((bf16[4,2,128]{2,1,0:T(2,128)(2,1)}), bf16[4,2,128]{2,1,0:T(2,128)(2,1)S(1)}, u32[]{:S(2)}, u32[]{:S(2)}) async-start(bf16[4,2,128]{2,1,0:T(2,128)(2,1)} %reshape.392), calls=%async_computation.3 | async-start | bytes 4096 | tf_op jit(solution)/shard_map/all_to_all | solution.py:193
  72.2 6.1 %slice-start.1 = ((bf16[1,32896]{1,0:T(2,128)(2,1)}), bf16[1,32768]{1,0:T(2,128)(2,1)S(1)}, s32[]{:S(2)}) async-start(bf16[1,32896]{1,0:T(2,128)(2,1)} %copy-done.3), calls=%async_computation.7 | async-start | bytes 262144 | tf_op jit(solution)/shard_map/slice | solution.py:39
  73.5 34.9 %all-to-all-start.4 = ((bf16[4,2,128]{2,1,0:T(2,128)(2,1)}), bf16[4,2,128]{2,1,0:T(2,128)(2,1)S(1)}, u32[]{:S(2)}, u32[]{:S(2)}) async-start(bf16[4,2,128]{2,1,0:T(2,128)(2,1)} %reshape.394), calls=%async_computation.4 | async-start | bytes 4096 | tf_op jit(solution)/shard_map/all_to_all | solution.py:192
  103.9 11.2 %copy-start.9 = (bf16[1,128,1024]{2,1,0:T(8,128)(2,1)S(1)}, bf16[1,128,1024]{2,1,0:T(8,128)(2,1)}, u32[]{:S(2)}) copy-start(bf16[1,128,1024]{2,1,0:T(8,128)(2,1)} %param.14) | copy-start | bytes 786436
  108.4 26.0 %all-to-all-start.2 = ((bf16[64,2,1024]{2,1,0:T(2,128)(2,1)}), bf16[64,2,1024]{2,1,0:T(2,128)(2,1)S(1)}, u32[]{:S(2)}, u32[]{:S(2)}) async-start(bf16[64,2,1024]{2,1,0:T(2,128)(2,1)} %reshape.390), calls=%async_computation.2 | async-start | bytes 524288 | tf_op jit(solution)/shard_map/all_to_all | solution.py:182
  115.0 231.8 %all-gather.3.cloned.1.call-start = ((), (), s32[]{:S(2)}) async-start(), calls=%async_computation.5 | async-start | bytes 4259840 | tf_op jit(solution)/shard_map/all_gather | solution.py:14
  135.7 0.8 copy-start.4
  136.4 6.4 %copy-start.1 = (f32[4,128,16,16]{1,3,2,0:T(8,128)}, f32[4,128,16,16]{1,3,2,0:T(8,128)S(1)}, u32[]{:S(2)}) copy-start(f32[4,128,16,16]{1,3,2,0:T(8,128)S(1)} %get-tuple-element.542) | copy-start | bytes 1572868 | tf_op jit(solution)/shard_map/while
  144.1 0.8 copy-start.6
  147.7 1.6 slice-start
  149.3 1.0 copy-start.2
  149.3 2.8 copy-start
  149.9 4.7 %copy-start.7 = (f32[4,16,16,16]{1,3,2,0:T(8,128)S(1)}, f32[4,16,16,16]{1,3,2,0:T(8,128)}, u32[]{:S(2)}) copy-start(f32[4,16,16,16]{1,3,2,0:T(8,128)} %copy-done.6) | copy-start | bytes 196612 | tf_op jit(solution)/shard_map/while
  154.6 6.4 %copy-start.1 = (f32[4,128,16,16]{1,3,2,0:T(8,128)}, f32[4,128,16,16]{1,3,2,0:T(8,128)S(1)}, u32[]{:S(2)}) copy-start(f32[4,128,16,16]{1,3,2,0:T(8,128)S(1)} %get-tuple-element.542) | copy-start | bytes 1572868 | tf_op jit(solution)/shard_map/while
  162.3 0.8 copy-start.6
  165.9 1.6 slice-start
  167.5 1.0 copy-start.2
  167.5 2.8 copy-start
  168.1 4.7 %copy-start.7 = (f32[4,16,16,16]{1,3,2,0:T(8,128)S(1)}, f32[4,16,16,16]{1,3,2,0:T(8,128)}, u32[]{:S(2)}) copy-start(f32[4,16,16,16]{1,3,2,0:T(8,128)} %copy-done.6) | copy-start | bytes 196612 | tf_op jit(solution)/shard_map/while
  172.8 6.4 %copy-start.1 = (f32[4,128,16,16]{1,3,2,0:T(8,128)}, f32[4,128,16,16]{1,3,2,0:T(8,128)S(1)}, u32[]{:S(2)}) copy-start(f32[4,128,16,16]{1,3,2,0:T(8,128)S(1)} %get-tuple-element.542) | copy-start | bytes 1572868 | tf_op jit(solution)/shard_map/while
  180.5 0.8 copy-start.6
  184.1 1.6 slice-start
  185.7 1.0 copy-start.2
  185.7 2.8 copy-start
  186.3 4.7 %copy-start.7 = (f32[4,16,16,16]{1,3,2,0:T(8,128)S(1)}, f32[4,16,16,16]{1,3,2,0:T(8,128)}, u32[]{:S(2)}) copy-start(f32[4,16,16,16]{1,3,2,0:T(8,128)} %copy-done.6) | copy-start | bytes 196612 | tf_op jit(solution)/shard_map/while
  191.0 6.4 %copy-start.1 = (f32[4,128,16,16]{1,3,2,0:T(8,128)}, f32[4,128,16,16]{1,3,2,0:T(8,128)S(1)}, u32[]{:S(2)}) copy-start(f32[4,128,16,16]{1,3,2,0:T(8,128)S(1)} %get-tuple-element.542) | copy-start | bytes 1572868 | tf_op jit(solution)/shard_map/while
  198.7 0.8 copy-start.6
  202.3 1.6 slice-start
  203.9 1.0 copy-start.2
  203.9 2.8 copy-start
  204.5 4.7 %copy-start.7 = (f32[4,16,16,16]{1,3,2,0:T(8,128)S(1)}, f32[4,16,16,16]{1,3,2,0:T(8,128)}, u32[]{:S(2)}) copy-start(f32[4,16,16,16]{1,3,2,0:T(8,128)} %copy-done.6) | copy-start | bytes 196612 | tf_op jit(solution)/shard_map/while
  346.8 90.0 %copy-start.5 = (f32[128,64,16]{0,2,1:T(8,128)S(1)}, f32[128,64,16]{0,2,1:T(8,128)}, u32[]{:S(2)}) copy-start(f32[128,64,16]{0,2,1:T(8,128)} %copy-done.4) | copy-start | bytes 1572868
  346.8 90.0 %copy-start.8 = (f32[4,128,16,16]{1,3,2,0:T(8,128)S(1)}, f32[4,128,16,16]{1,3,2,0:T(8,128)}, u32[]{:S(2)}) copy-start(f32[4,128,16,16]{1,3,2,0:T(8,128)} %get-tuple-element.256) | copy-start | bytes 1572868
  346.8 90.0 %copy-start.10 = (f32[1024]{0:T(1024)S(1)}, f32[1024]{0:T(1024)}, u32[]{:S(2)}) copy-start(f32[1024]{0:T(1024)} %param.21) | copy-start | bytes 12292
Sparse Core Ops, SparseCore 0:
  210.2 136.5 all-gather.2
where the time goes:
time: 451 us; the launch traced here: 445 us
  blocking collectives  97.8 us (22%)
  local copies, waits for them, and re-layouts  87.2 us (19%)
  other arithmetic  85.1 us (19%)
  waiting for transfers between devices  71.6 us (16%)
  matrix products  48.3 us (11%)
  starting transfers between devices  37.6 us (8%)
  between operations  13.9 us (3%)
    all_gather x1, blocking collectives, entering_2(): everything = jax.tree.map(lambda part: lax.all_gather(part, axis), array)  97.8 us
    select_n x64, other arithmetic, turn(): return jax.tree.map(lambda a, b: jnp.where(reached, a, b), new, before)  56.6 us
    all_gather x1, waiting for transfers between devices, entering_2(): everything = jax.tree.map(lambda part: lax.all_gather(part, axis), array)  37.4 us
    mul x192, local copies, waits for them, and re-layouts, merge_carry(): moved = (decay_second[:, :, None] * spread).reshape(state_first.shape)  29.9 us
    all_to_all x1, starting transfers between devices, body(): lax.all_to_all(outgoing, 'ctx', split_axis=0, concat_axis=0, tiled=True)  18.7 us
    all_to_all x1, waiting for transfers between devices, body(): lax.all_to_all(medium.reshape(ctx_size, tokens * channels), 'ctx', split_...  18 us
    dot_general x16, matrix products, apply_part(): jnp.einsum('ngtj,njgc->ntgc', masked, window_part, preferred_element_type...  17.6 us
    all_to_all x1, waiting for transfers between devices, body(): lax.all_to_all(outgoing, 'ctx', split_axis=0, concat_axis=0, tiled=True)  16.2 us
  transfers between devices with their start and end apart: 6, of which 3 were waited for; matrix products, arithmetic and copies ran while one was open for 12% of the time, Pallas kernels for 0%

commit v1 on v0

v1 whole, which is shorter than its diff:
```python
import functools

import jax
import jax.numpy as jnp
from jax import lax
from jax.experimental import pallas as pl
from jax.experimental.pallas import tpu as pltpu
from jax.sharding import PartitionSpec as P

MESH = pl.DeviceIdType.MESH
CH = 16
MODES = 16
TOK = 128
LANES = 256
GB = LANES // CH
NB = 4
WIDE = NB * LANES
GROUPS = WIDE // CH
CTX = 64

f32 = jnp.float32
bf16 = jnp.bfloat16


def iota(shape, dim):
    return lax.broadcasted_iota(jnp.int32, shape, dim)


def one_hot(cond):
    return jnp.where(cond, 1.0, 0.0).astype(bf16)


def dot(a, b):
    return jnp.dot(a, b, preferred_element_type=f32)


def minus_expm1_neg(x):
    series = x * (1.0 - x * (0.5 - x * (1.0 / 6 - x * (1.0 / 24 - x * (1.0 / 120 - x * (1.0 / 720))))))
    return jnp.where(x < 0.125, series, 1.0 - jnp.exp(-x))


def scaled_of(rate, residue):
    return residue * jnp.sqrt(minus_expm1_neg(2.0 * rate) * (1.0 / MODES))


def kernel(
    q_hbm, k_hbm, v_hbm, starts, taps_hbm, rate_hbm, residue_hbm, skip, out,
    q_buf, k_buf, v_buf, window, tapbuf, ratebuf, resbuf, line, hline, toep, modal, ends, carry,
    gated, partial, e_buf, recv, prefix, states,
    in_sem, halo_send, halo_recv, tap_send, tap_recv, mod_send, mod_recv, p1_send, p1_recv, p2_send, p2_recv,
):
    fs = lax.axis_index("fsdp")
    cx = lax.axis_index("ctx")
    dp = lax.axis_index("dp")

    loads = [
        pltpu.make_async_copy(k_hbm.at[0], k_buf, in_sem.at[0]),
        pltpu.make_async_copy(v_hbm.at[0], v_buf, in_sem.at[1]),
        pltpu.make_async_copy(q_hbm.at[0], q_buf, in_sem.at[2]),
    ]
    for load in loads:
        load.start()

    barrier = pltpu.get_barrier_semaphore()

    def greet(d, c):
        pl.semaphore_signal(
            barrier, inc=1, device_id=(fs, lax.rem(cx + d, CTX), dp), device_id_type=MESH
        )
        return c

    lax.fori_loop(1, CTX, greet, 0)
    pl.semaphore_signal(barrier, inc=1, device_id=(1 - fs, cx, dp), device_id_type=MESH)
    for d in (1, 2, 3):
        pl.semaphore_signal(
            barrier, inc=1, device_id=(fs, cx, lax.rem(dp + d, 4)), device_id_type=MESH
        )

    own_row = starts[pl.ds(cx, 1), :].astype(f32)
    before_row = starts[pl.ds(lax.rem(cx + CTX - 1, CTX), 1), :].astype(f32)
    both = jnp.concatenate([before_row, own_row], axis=1)
    t_of = iota((TOK, 2 * TOK), 0)
    s_of = iota((TOK, 2 * TOK), 1)
    at_row = jnp.sum(jnp.where(s_of <= t_of + TOK, both, 0.0), axis=1, keepdims=True)
    upper = one_hot(iota((2 * TOK, 2 * TOK), 0) <= iota((2 * TOK, 2 * TOK), 1))
    counts = dot(jnp.broadcast_to(both, (8, 2 * TOK)).astype(bf16), upper)[0:1]
    first = jnp.where(cx == 0, TOK, 0)
    mask = jnp.where((at_row == counts) & (s_of <= t_of + TOK) & (s_of >= first), 1.0, 0.0)
    before = jnp.sum(before_row, axis=1, keepdims=True)
    total = before + jnp.sum(own_row, axis=1, keepdims=True)
    keep = jnp.where(counts[:, TOK:] == total, 1.0, 0.0)
    continues = jnp.where(at_row == before, 1.0, 0.0)

    loads[0].wait()
    loads[1].wait()
    for j in range(NB):
        cols = pl.ds(j * LANES, LANES)
        window[j, TOK:, :] = (k_buf[:, cols].astype(f32) * v_buf[:, cols].astype(f32)).astype(bf16)

    @pl.when(cx == 0)
    def _():
        for j in range(NB):
            window[j, :TOK, :] = jnp.zeros((TOK, LANES), bf16)

    pl.semaphore_wait(barrier, CTX - 1 + 4)

    halos = [
        pltpu.make_async_remote_copy(
            window.at[j, pl.ds(TOK, TOK)], window.at[j, pl.ds(0, TOK)], halo_send.at[j], halo_recv.at[j],
            device_id=(fs, lax.rem(cx + 1, CTX), dp), device_id_type=MESH,
        )
        for j in range(NB)
    ]

    @pl.when(cx < CTX - 1)
    def _():
        for halo in halos:
            halo.start()

    other = pl.multiple_of(((1 - fs) * 4 + dp) * GROUPS, GROUPS)
    mine = pl.multiple_of((fs * 4 + dp) * GROUPS, GROUPS)
    tap_copy = pltpu.make_async_remote_copy(
        taps_hbm.at[pl.ds(other, GROUPS)], tapbuf.at[fs], tap_send, tap_recv,
        device_id=(1 - fs, cx, dp), device_id_type=MESH,
    )
    tap_copy.start()
    tap_own = pltpu.make_async_copy(taps_hbm.at[pl.ds(mine, GROUPS)], tapbuf.at[fs], in_sem.at[3])
    tap_own.start()
    modal_copies = []
    for d in (1, 2, 3):
        to = lax.rem(dp + d, 4)
        rows = pl.ds(pl.multiple_of(to * GROUPS, GROUPS), GROUPS)
        for i, (src, dst) in enumerate(((rate_hbm, ratebuf), (residue_hbm, resbuf))):
            copy = pltpu.make_async_remote_copy(
                src.at[rows], dst.at[dp], mod_send.at[i, d - 1], mod_recv.at[i, d - 1],
                device_id=(fs, cx, to), device_id_type=MESH,
            )
            copy.start()
            modal_copies.append(copy)
    rows = pl.ds(pl.multiple_of(dp * GROUPS, GROUPS), GROUPS)
    rate_own = pltpu.make_async_copy(rate_hbm.at[rows], ratebuf.at[dp], in_sem.at[4])
    residue_own = pltpu.make_async_copy(residue_hbm.at[rows], resbuf.at[dp], in_sem.at[5])
    rate_own.start()
    residue_own.start()

    tap_own.wait()
    tap_copy.wait()
    flip = [one_hot(iota((TOK // 2, 2 * TOK), 1) == TOK - h * (TOK // 2) - iota((TOK // 2, 2 * TOK), 0)) for h in (0, 1)]
    line[...] = dot(tapbuf[0], flip[0]) + dot(tapbuf[1], flip[1])

    def build_medium(g, c):
        row = jnp.broadcast_to(line[pl.ds(g, 1), :], (TOK, 2 * TOK))
        toep[g] = (pltpu.roll(row, 0, 1, stride=1, stride_axis=0) * mask).astype(bf16)
        return c

    lax.fori_loop(0, GROUPS, build_medium, 0)

    rate_own.wait()
    residue_own.wait()
    for copy in modal_copies:
        copy.wait()

    def gather_modes(buf):
        parts = [dot(buf[d], one_hot(iota((4, MODES), 1) == 4 * d + iota((4, MODES), 0))) for d in range(4)]
        return (parts[0] + parts[1]) + (parts[2] + parts[3])

    rate16 = gather_modes(ratebuf)
    res16 = gather_modes(resbuf)
    repeat = one_hot(iota((GROUPS * MODES, GROUPS), 0) // MODES == iota((GROUPS * MODES, GROUPS), 1))
    own_mode = iota((GROUPS * MODES, MODES), 0) % MODES == iota((GROUPS * MODES, MODES), 1)
    ones = jnp.ones((MODES, TOK), bf16)

    def column(per_group):
        spread = jnp.where(own_mode, dot(repeat, per_group.astype(bf16)), 0.0)
        return dot(spread.astype(bf16), ones)

    rate_col = column(rate16)
    scaled_col = scaled_of(rate_col, column(res16))
    lag = ((TOK - iota((1, TOK), 1)) % TOK).astype(f32)
    powers = jnp.exp(-rate_col * lag)
    hline[...] = jnp.sum((powers * scaled_col).reshape(GROUPS, MODES, TOK), axis=1)
    ends[...] = (pltpu.roll(powers, TOK - 1, 1) * keep).astype(bf16)

    def build_modal(g, c):
        row = jnp.broadcast_to(hline[pl.ds(g, 1), :], (TOK, TOK))
        modal[g] = (pltpu.roll(row, 0, 1, stride=1, stride_axis=0) * mask[:, TOK:]).astype(bf16)
        return c

    lax.fori_loop(0, GROUPS, build_modal, 0)

    tile = one_hot(iota((MODES, GROUPS * MODES), 1) % MODES == iota((MODES, GROUPS * MODES), 0))
    own_group = iota((GROUPS, GROUPS * MODES), 1) // MODES == iota((GROUPS, GROUPS * MODES), 0)

    def as_row(per_group):
        spread = jnp.where(own_group, dot(per_group.astype(bf16), tile), 0.0)
        return jnp.sum(spread, axis=0, keepdims=True)

    rate_row = as_row(rate16)
    scaled_row = scaled_of(rate_row, as_row(res16))
    steps = (iota((TOK, 1), 0) + 1).astype(f32)
    carry[...] = (jnp.exp(-rate_row * steps) * scaled_row * continues).astype(bf16)

    med_mode = lax.rem(cx, MODES)
    med_block = cx // MODES
    rate_mode = jnp.sum(jnp.where(iota((GROUPS, MODES), 1) == med_mode, rate16, 0.0), axis=1, keepdims=True)
    group_of = med_block * GB + iota((GROUPS, LANES), 1) // CH
    rate_med = jnp.sum(jnp.where(group_of == iota((GROUPS, LANES), 0), rate_mode, 0.0), axis=0, keepdims=True)
    no_start = jnp.where(jnp.sum(starts[...], axis=1, keepdims=True) == 0, 1.0, 0.0)
    a = jnp.exp(-rate_med * TOK) * no_start
    place = iota((CTX, 1), 0)
    scales = []
    for step in (1, 2, 4, 8, 16, 32):
        a = jnp.where(place >= step, a, 0.0)
        scales.append(a)
        a = a * pltpu.roll(a, step, 0)

    loads[2].wait()
    lane_group = iota((1, LANES), 1) // CH

    for j in range(NB):
        @pl.when(cx > 0)
        def _():
            halos[j].wait_recv()

        data = window[j]
        groups = [dot(toep[j * GB + i], data) for i in range(GB)]
        medium = groups[0]
        for i in range(1, GB):
            medium = jnp.where(lane_group == i, groups[i], medium)
        value = (q_buf[:, j * LANES:(j + 1) * LANES].astype(f32) * medium.astype(bf16).astype(f32)).astype(bf16)
        gated[j] = value
        full = dot(ends[pl.ds(j * GB * MODES, GB * MODES), :], value)
        state = full[0:MODES]
        for i in range(1, GB):
            state = jnp.where(lane_group == i, full[i * MODES:(i + 1) * MODES], state)
        e_buf[j] = state

        def send_one(n, c):
            to = j * MODES + n

            @pl.when(to != cx)
            def _():
                pltpu.make_async_remote_copy(
                    e_buf.at[j, pl.ds(n, 1)], recv.at[pl.ds(cx, 1)], p1_send, p1_recv,
                    device_id=(fs, to, dp), device_id_type=MESH,
                ).start()

            @pl.when(to == cx)
            def _():
                pltpu.make_async_copy(e_buf.at[j, pl.ds(n, 1)], recv.at[pl.ds(cx, 1)], p1_recv).start()

            return c

        lax.fori_loop(0, MODES, send_one, 0)

    for j in range(NB):
        value = gated[j]
        groups = [dot(modal[j * GB + i], value) for i in range(GB)]
        inside = groups[0]
        for i in range(1, GB):
            inside = jnp.where(lane_group == i, groups[i], inside)
        partial[j] = inside + skip[:, j * LANES:(j + 1) * LANES] * value.astype(f32)

    pltpu.make_async_copy(recv, recv, p1_recv).wait()
    b = recv[...]
    for step, scale in zip((1, 2, 4, 8, 16, 32), scales):
        b = b + scale * pltpu.roll(b, step, 0)
    prefix[...] = jnp.where(place == 0, 0.0, pltpu.roll(b, 1, 0))

    def return_one(d, c):
        to = lax.rem(cx + d, CTX)
        pltpu.make_async_remote_copy(
            prefix.at[pl.ds(to, 1)], states.at[med_block, pl.ds(med_mode, 1)], p2_send, p2_recv.at[med_block],
            device_id=(fs, to, dp), device_id_type=MESH,
        ).start()
        return c

    pltpu.make_async_copy(prefix.at[pl.ds(cx, 1)], states.at[med_block, pl.ds(med_mode, 1)], p2_recv.at[med_block]).start()
    lax.fori_loop(1, CTX, return_one, 0)

    diagonal = iota((LANES, LANES), 0) // MODES == iota((LANES, LANES), 1) // CH
    for j in range(NB):
        pltpu.make_async_copy(states.at[j], states.at[j], p2_recv.at[j]).wait()
        spread = jnp.where(diagonal, jnp.concatenate([states[j]] * GB, axis=0), 0.0).astype(bf16)
        carried = dot(carry[:, j * LANES:(j + 1) * LANES], spread)
        out[0, :, j * LANES:(j + 1) * LANES] = (partial[j] + carried).astype(bf16)

    @pl.when(cx < CTX - 1)
    def _():
        for halo in halos:
            halo.wait_send()

    for sem in (p1_send, p2_send):
        pltpu.make_async_copy(prefix.at[pl.ds(0, 56)], prefix.at[pl.ds(0, 56)], sem).wait()

        def drain(i, c):
            pltpu.make_async_copy(prefix.at[pl.ds(i, 1)], prefix.at[pl.ds(i, 1)], sem).wait()
            return c

        lax.fori_loop(0, 7, drain, 0)


def body(query, key, value, starts, taps, rate, residue, skip):
    any_space = pl.BlockSpec(memory_space=pl.ANY)
    vmem = pl.BlockSpec(memory_space=pltpu.VMEM)
    dma = pltpu.SemaphoreType.DMA
    return pl.pallas_call(
        kernel,
        out_shape=jax.ShapeDtypeStruct((1, TOK, WIDE), bf16),
        in_specs=[any_space] * 3 + [vmem] + [any_space] * 3 + [vmem],
        out_specs=vmem,
        scratch_shapes=[
            pltpu.VMEM((TOK, WIDE), bf16),
            pltpu.VMEM((TOK, WIDE), bf16),
            pltpu.VMEM((TOK, WIDE), bf16),
            pltpu.VMEM((NB, 2 * TOK, LANES), bf16),
            pltpu.VMEM((2, GROUPS, TOK // 2), bf16),
            pltpu.VMEM((4, GROUPS, 4), bf16),
            pltpu.VMEM((4, GROUPS, 4), bf16),
            pltpu.VMEM((GROUPS, 2 * TOK), f32),
            pltpu.VMEM((GROUPS, TOK), f32),
            pltpu.VMEM((GROUPS, TOK, 2 * TOK), bf16),
            pltpu.VMEM((GROUPS, TOK, TOK), bf16),
            pltpu.VMEM((GROUPS * MODES, TOK), bf16),
            pltpu.VMEM((TOK, GROUPS * MODES), bf16),
            pltpu.VMEM((NB, TOK, LANES), bf16),
            pltpu.VMEM((NB, TOK, LANES), f32),
            pltpu.VMEM((NB, MODES, LANES), f32),
            pltpu.VMEM((CTX, LANES), f32),
            pltpu.VMEM((CTX, LANES), f32),
            pltpu.VMEM((NB, MODES, LANES), f32),
            dma((6,)), dma((NB,)), dma((NB,)), dma, dma, dma((2, 3)), dma((2, 3)),
            dma, dma, dma, dma((NB,)),
        ],
        compiler_params=pltpu.CompilerParams(
            collective_id=1, has_side_effects=True, vmem_limit_bytes=48 * 1024 * 1024
        ),
    )(query, key, value, starts.reshape(CTX, TOK), taps, rate, residue, skip.reshape(1, WIDE))


def solution(mesh):
    return jax.shard_map(
        body,
        mesh=mesh,
        in_specs=(
            P(None, "ctx", ("fsdp", "dp")),
            P(None, "ctx", ("fsdp", "dp")),
            P(None, "ctx", ("fsdp", "dp")),
            P(),
            P(None, "fsdp"),
            P("fsdp", "dp"),
            P("fsdp", "dp"),
            P(("fsdp", "dp")),
        ),
        out_specs=P(None, "ctx", ("fsdp", "dp")),
        check_vma=False,
    )
```

time: 451 us -> 59.2 us (0.13)
  the two profiles are of different devices: /device:TPU:24 before, /device:TPU:2 now
where the time goes in v1:
time: 59.2 us; the launch traced here: 58.9 us
  Pallas kernels  53.6 us (91%)
  local copies, waits for them, and re-layouts  5.23 us (9%)
    pallas_call x1, Pallas kernels, body(): pl.pallas_call(kernel, out_shape=jax.ShapeDtypeStruct((1, TOK, WIDE), bf1...  53.6 us
    unnamed x16, local copies, waits for them, and re-layouts  5.23 us

profile of v1, /device:TPU:2, one launch (start us, length us, event | category | flops | bytes accessed | tf_op | source)
XLA Modules:
  0.0 58.9 jit_solution(13467111291576824296)
XLA Ops:
  0.0 0.0 copy-start.5
  0.0 0.0 copy-start
  0.0 0.7 %copy-done.5 = bf16[256,4]{0,1:T(4,128)(2,1)S(1)} copy-done((bf16[256,4]{0,1:T(4,128)(2,1)S(1)}, bf16[256,4]{0,1:T(4,128)(2,1)}, u32[]{:S(2)}) %copy-start.5) | copy-done | bytes 2072
  0.7 0.1 copy.10.rate_hbm
  0.8 0.8 %copy.11.residue_hbm = bf16[256,4]{1,0:T(8,128)(2,1)S(1)} copy(bf16[256,4]{0,1:T(4,128)(2,1)} %param.14) | data formatting | bytes 4096 | tf_op args[6]
  1.6 0.0 copy-start.3
  1.7 0.0 copy-start.4
  1.7 1.0 %copy.9.taps_hbm = bf16[512,64]{1,0:T(8,128)(2,1)S(1)} copy(bf16[512,64]{0,1:T(8,128)(2,1)} %param.12) | data formatting | bytes 131072 | tf_op args[4]
  2.6 0.0 copy-done
  2.7 0.0 copy-done.3
  2.7 0.0 copy-done.4
  2.7 0.0 copy-start.1
  2.7 0.9 %copy-done.1 = bf16[1,128,1024]{2,1,0:T(8,128)(2,1)S(1)} copy-done((bf16[1,128,1024]{2,1,0:T(8,128)(2,1)S(1)}, bf16[1,128,1024]{2,1,0:T(8,128)(2,1)}, u32[]{:S(2)}) %copy-start.1) | copy-done | bytes 262168
  3.6 0.0 copy-start.2
  3.6 0.9 %copy-done.2 = bf16[1,128,1024]{2,1,0:T(8,128)(2,1)S(1)} copy-done((bf16[1,128,1024]{2,1,0:T(8,128)(2,1)S(1)}, bf16[1,128,1024]{2,1,0:T(8,128)(2,1)}, u32[]{:S(2)}) %copy-start.2) | copy-done | bytes 262168
  4.6 53.6 %shard_map.82 = bf16[1,128,1024]{2,1,0:T(8,128)(2,1)S(1)} custom-call(bf16[1,128,1024]{2,1,0:T(8,128)(2,1)S(1)} %copy-done, bf16[1,128,1024]{2,1,0:T(8,128)(2,1)S(1)} %copy-done.1, bf16[1,128,1024]{2,1,0:T(8,128)(2,1)S(1)} %copy-done.2, s32[64,128]{1,0:T(8,128)S(1)} %bitcast.2, bf16[512,64]{1,0:T(8,128)(2,1)S(1)} %copy.9.taps_hbm, ...), custom_call_target="tpu_custom_call" | custom-call | tf_op jit(solution)/shard_map/pallas_call | solution.py:307
  58.2 0.7 %copy.13 = bf16[1,128,1024]{2,1,0:T(8,128)(2,1)} copy(bf16[1,128,1024]{2,1,0:T(8,128)(2,1)S(1)} %shard_map.82) | data formatting | bytes 524288
Async XLA Ops:
  0.0 0.7 %copy-start.5 = (bf16[256,4]{0,1:T(4,128)(2,1)S(1)}, bf16[256,4]{0,1:T(4,128)(2,1)}, u32[]{:S(2)}) copy-start(bf16[256,4]{0,1:T(4,128)(2,1)} %param.13) | copy-start | bytes 6148
  0.0 2.6 %copy-start = (bf16[1,128,1024]{2,1,0:T(8,128)(2,1)S(1)}, bf16[1,128,1024]{2,1,0:T(8,128)(2,1)}, u32[]{:S(2)}) copy-start(bf16[1,128,1024]{2,1,0:T(8,128)(2,1)} %q_hbm.1) | copy-start | bytes 786436
  1.6 1.0 %copy-start.3 = (s32[1,8192]{1,0:T(1,128)S(1)}, s32[1,8192]{1,0:T(1,128)}, u32[]{:S(2)}) copy-start(s32[1,8192]{1,0:T(1,128)} %param.11) | copy-start | bytes 98308
  1.7 1.0 %copy-start.4 = (f32[1024]{0:T(1024)S(1)}, f32[1024]{0:T(1024)}, u32[]{:S(2)}) copy-start(f32[1024]{0:T(1024)} %param.15) | copy-start | bytes 12292
  2.7 1.0 %copy-start.1 = (bf16[1,128,1024]{2,1,0:T(8,128)(2,1)S(1)}, bf16[1,128,1024]{2,1,0:T(8,128)(2,1)}, u32[]{:S(2)}) copy-start(bf16[1,128,1024]{2,1,0:T(8,128)(2,1)} %k_hbm.1) | copy-start | bytes 786436
  3.6 0.9 %copy-start.2 = (bf16[1,128,1024]{2,1,0:T(8,128)(2,1)S(1)}, bf16[1,128,1024]{2,1,0:T(8,128)(2,1)}, u32[]{:S(2)}) copy-start(bf16[1,128,1024]{2,1,0:T(8,128)(2,1)} %v_hbm.1) | copy-start | bytes 786436

commit v2 on v1

--- a/solution.py
+++ b/solution.py
@@ -16,7 +16,10 @@
 NB = 4
 WIDE = NB * LANES
 GROUPS = WIDE // CH
+PAIR = 2 * GROUPS
 CTX = 64
+STRIP = 16
+STRIPS = TOK // STRIP
 
 f32 = jnp.float32
 bf16 = jnp.bfloat16
@@ -32,6 +35,10 @@
 
 def dot(a, b):
     return jnp.dot(a, b, preferred_element_type=f32)
+
+
+def dot_rows(a, b):
+    return lax.dot_general(a, b, (((0,), (0,)), ((), ())), preferred_element_type=f32)
 
 
 def minus_expm1_neg(x):
@@ -95,7 +102,9 @@
     loads[1].wait()
     for j in range(NB):
         cols = pl.ds(j * LANES, LANES)
-        window[j, TOK:, :] = (k_buf[:, cols].astype(f32) * v_buf[:, cols].astype(f32)).astype(bf16)
+        window[j, TOK:2 * TOK, :] = (k_buf[:, cols].astype(f32) * v_buf[:, cols].astype(f32)).astype(bf16)
+        window[j, 2 * TOK:, :] = jnp.zeros((TOK, LANES), bf16)
+        gated[j, :TOK - STRIP, :] = jnp.zeros((TOK - STRIP, LANES), bf16)
 
     @pl.when(cx == 0)
     def _():
@@ -117,43 +126,55 @@
         for halo in halos:
             halo.start()
 
-    other = pl.multiple_of(((1 - fs) * 4 + dp) * GROUPS, GROUPS)
-    mine = pl.multiple_of((fs * 4 + dp) * GROUPS, GROUPS)
+    half = lax.rem(dp, 2) * GROUPS
+    other = pl.multiple_of(((1 - fs) * 2 + dp // 2) * PAIR, PAIR)
+    mine = pl.multiple_of((fs * 2 + dp // 2) * PAIR, PAIR)
     tap_copy = pltpu.make_async_remote_copy(
-        taps_hbm.at[pl.ds(other, GROUPS)], tapbuf.at[fs], tap_send, tap_recv,
+        taps_hbm.at[:, pl.ds(other, PAIR)], tapbuf.at[fs], tap_send, tap_recv,
         device_id=(1 - fs, cx, dp), device_id_type=MESH,
     )
     tap_copy.start()
-    tap_own = pltpu.make_async_copy(taps_hbm.at[pl.ds(mine, GROUPS)], tapbuf.at[fs], in_sem.at[3])
+    tap_own = pltpu.make_async_copy(taps_hbm.at[:, pl.ds(mine, PAIR)], tapbuf.at[fs], in_sem.at[3])
     tap_own.start()
     modal_copies = []
     for d in (1, 2, 3):
         to = lax.rem(dp + d, 4)
-        rows = pl.ds(pl.multiple_of(to * GROUPS, GROUPS), GROUPS)
+        pair = pl.ds(pl.multiple_of(to // 2 * PAIR, PAIR), PAIR)
         for i, (src, dst) in enumerate(((rate_hbm, ratebuf), (residue_hbm, resbuf))):
             copy = pltpu.make_async_remote_copy(
-                src.at[rows], dst.at[dp], mod_send.at[i, d - 1], mod_recv.at[i, d - 1],
+                src.at[:, pair], dst.at[dp], mod_send.at[i, d - 1], mod_recv.at[i, d - 1],
                 device_id=(fs, cx, to), device_id_type=MESH,
             )
             copy.start()
             modal_copies.append(copy)
-    rows = pl.ds(pl.multiple_of(dp * GROUPS, GROUPS), GROUPS)
-    rate_own = pltpu.make_async_copy(rate_hbm.at[rows], ratebuf.at[dp], in_sem.at[4])
-    residue_own = pltpu.make_async_copy(residue_hbm.at[rows], resbuf.at[dp], in_sem.at[5])
+    pair = pl.ds(pl.multiple_of(dp // 2 * PAIR, PAIR), PAIR)
+    rate_own = pltpu.make_async_copy(rate_hbm.at[:, pair], ratebuf.at[dp], in_sem.at[4])
+    residue_own = pltpu.make_async_copy(residue_hbm.at[:, pair], resbuf.at[dp], in_sem.at[5])
     rate_own.start()
     residue_own.start()
 
     tap_own.wait()
     tap_copy.wait()
     flip = [one_hot(iota((TOK // 2, 2 * TOK), 1) == TOK - h * (TOK // 2) - iota((TOK // 2, 2 * TOK), 0)) for h in (0, 1)]
-    line[...] = dot(tapbuf[0], flip[0]) + dot(tapbuf[1], flip[1])
+    line[...] = dot_rows(tapbuf[0], flip[0]) + dot_rows(tapbuf[1], flip[1])
+
+    wide_lane = iota((STRIP, 2 * TOK), 1)
+    wide_masks = []
+    for a in range(STRIPS):
+        part = mask[a * STRIP:(a + 1) * STRIP]
+        if a:
+            part = pltpu.roll(part, 2 * TOK - a * STRIP, 1)
+        wide_masks.append(jnp.where(wide_lane < TOK + STRIP, part, 0.0).astype(bf16))
 
     def build_medium(g, c):
-        row = jnp.broadcast_to(line[pl.ds(g, 1), :], (TOK, 2 * TOK))
-        toep[g] = (pltpu.roll(row, 0, 1, stride=1, stride_axis=0) * mask).astype(bf16)
+        row = jnp.broadcast_to(line[pl.ds(half + g, 1), :], (STRIP, 2 * TOK))
+        base = pltpu.roll(row, 0, 1, stride=1, stride_axis=0).astype(bf16)
+        at = pl.ds(pl.multiple_of((g & 15) * STRIP, STRIP), STRIP)
+        for a in range(STRIPS):
+            toep[(g >> 4) * STRIPS + a, at, :] = base * wide_masks[a]
         return c
 
-    lax.fori_loop(0, GROUPS, build_medium, 0)
+    lax.fori_loop(0, GROUPS, build_medium, 0, unroll=8)
 
     rate_own.wait()
     residue_own.wait()
@@ -161,13 +182,13 @@
         copy.wait()
 
     def gather_modes(buf):
-        parts = [dot(buf[d], one_hot(iota((4, MODES), 1) == 4 * d + iota((4, MODES), 0))) for d in range(4)]
+        parts = [dot_rows(buf[d], one_hot(iota((4, MODES), 1) == 4 * d + iota((4, MODES), 0))) for d in range(4)]
         return (parts[0] + parts[1]) + (parts[2] + parts[3])
 
     rate16 = gather_modes(ratebuf)
     res16 = gather_modes(resbuf)
-    repeat = one_hot(iota((GROUPS * MODES, GROUPS), 0) // MODES == iota((GROUPS * MODES, GROUPS), 1))
-    own_mode = iota((GROUPS * MODES, MODES), 0) % MODES == iota((GROUPS * MODES, MODES), 1)
+    repeat = one_hot(half + (iota((GROUPS * MODES, PAIR), 0) >> 4) == iota((GROUPS * MODES, PAIR), 1))
+    own_mode = (iota((GROUPS * MODES, MODES), 0) & 15) == iota((GROUPS * MODES, MODES), 1)
     ones = jnp.ones((MODES, TOK), bf16)
 
     def column(per_group):
@@ -176,20 +197,32 @@
 
     rate_col = column(rate16)
     scaled_col = scaled_of(rate_col, column(res16))
-    lag = ((TOK - iota((1, TOK), 1)) % TOK).astype(f32)
+    lag = ((TOK - STRIP - iota((1, TOK), 1)) & (TOK - 1)).astype(f32)
     powers = jnp.exp(-rate_col * lag)
     hline[...] = jnp.sum((powers * scaled_col).reshape(GROUPS, MODES, TOK), axis=1)
-    ends[...] = (pltpu.roll(powers, TOK - 1, 1) * keep).astype(bf16)
+    ends[...] = (pltpu.roll(powers, STRIP - 1, 1) * keep).astype(bf16)
+
+    lane = iota((STRIP, TOK), 1)
+    masks = []
+    for a in range(STRIPS):
+        part = mask[a * STRIP:(a + 1) * STRIP, TOK:]
+        shift = TOK - STRIP - a * STRIP
+        if shift:
+            part = jnp.where(lane >= shift, pltpu.roll(part, shift, 1), 0.0)
+        masks.append(part.astype(bf16))
 
     def build_modal(g, c):
-        row = jnp.broadcast_to(hline[pl.ds(g, 1), :], (TOK, TOK))
-        modal[g] = (pltpu.roll(row, 0, 1, stride=1, stride_axis=0) * mask[:, TOK:]).astype(bf16)
+        row = jnp.broadcast_to(hline[pl.ds(g, 1), :], (STRIP, TOK))
+        base = pltpu.roll(row, 0, 1, stride=1, stride_axis=0).astype(bf16)
+        at = pl.ds(pl.multiple_of((g & 15) * STRIP, STRIP), STRIP)
+        for a in range(STRIPS):
+            modal[(g >> 4) * STRIPS + a, at, :] = base * masks[a]
         return c
 
-    lax.fori_loop(0, GROUPS, build_modal, 0)
-
-    tile = one_hot(iota((MODES, GROUPS * MODES), 1) % MODES == iota((MODES, GROUPS * MODES), 0))
-    own_group = iota((GROUPS, GROUPS * MODES), 1) // MODES == iota((GROUPS, GROUPS * MODES), 0)
+    lax.fori_loop(0, GROUPS, build_modal, 0, unroll=8)
+
+    tile = one_hot((iota((MODES, GROUPS * MODES), 1) & 15) == iota((MODES, GROUPS * MODES), 0))
+    own_group = half + (iota((PAIR, GROUPS * MODES), 1) >> 4) == iota((PAIR, GROUPS * MODES), 0)
 
     def as_row(per_group):
         spread = jnp.where(own_group, dot(per_group.astype(bf16), tile), 0.0)
@@ -202,9 +235,9 @@
 
     med_mode = lax.rem(cx, MODES)
     med_block = cx // MODES
-    rate_mode = jnp.sum(jnp.where(iota((GROUPS, MODES), 1) == med_mode, rate16, 0.0), axis=1, keepdims=True)
-    group_of = med_block * GB + iota((GROUPS, LANES), 1) // CH
-    rate_med = jnp.sum(jnp.where(group_of == iota((GROUPS, LANES), 0), rate_mode, 0.0), axis=0, keepdims=True)
+    rate_mode = jnp.sum(jnp.where(iota((PAIR, MODES), 1) == med_mode, rate16, 0.0), axis=1, keepdims=True)
+    group_of = half + med_block * GB + (iota((PAIR, LANES), 1) >> 4)
+    rate_med = jnp.sum(jnp.where(group_of == iota((PAIR, LANES), 0), rate_mode, 0.0), axis=0, keepdims=True)
     no_start = jnp.where(jnp.sum(starts[...], axis=1, keepdims=True) == 0, 1.0, 0.0)
     a = jnp.exp(-rate_med * TOK) * no_start
     place = iota((CTX, 1), 0)
@@ -215,25 +248,26 @@
         a = a * pltpu.roll(a, step, 0)
 
     loads[2].wait()
-    lane_group = iota((1, LANES), 1) // CH
+    lane_group = iota((1, LANES), 1) >> 4
+
+    def pick(rows, size):
+        out_rows = rows[:size]
+        for i in range(1, GB):
+            out_rows = jnp.where(lane_group == i, rows[i * size:(i + 1) * size], out_rows)
+        return out_rows
 
     for j in range(NB):
         @pl.when(cx > 0)
         def _():
             halos[j].wait_recv()
 
-        data = window[j]
-        groups = [dot(toep[j * GB + i], data) for i in range(GB)]
-        medium = groups[0]
-        for i in range(1, GB):
-            medium = jnp.where(lane_group == i, groups[i], medium)
+        medium = jnp.concatenate(
+            [pick(dot(toep[j * STRIPS + a], window[j, a * STRIP:a * STRIP + 2 * TOK, :]), STRIP) for a in range(STRIPS)], axis=0
+        )
         value = (q_buf[:, j * LANES:(j + 1) * LANES].astype(f32) * medium.astype(bf16).astype(f32)).astype(bf16)
-        gated[j] = value
+        gated[j, TOK - STRIP:, :] = value
         full = dot(ends[pl.ds(j * GB * MODES, GB * MODES), :], value)
-        state = full[0:MODES]
-        for i in range(1, GB):
-            state = jnp.where(lane_group == i, full[i * MODES:(i + 1) * MODES], state)
-        e_buf[j] = state
+        e_buf[j] = pick(full, MODES)
 
         def send_one(n, c):
             to = j * MODES + n
@@ -254,11 +288,10 @@
         lax.fori_loop(0, MODES, send_one, 0)
 
     for j in range(NB):
-        value = gated[j]
-        groups = [dot(modal[j * GB + i], value) for i in range(GB)]
-        inside = groups[0]
-        for i in range(1, GB):
-            inside = jnp.where(lane_group == i, groups[i], inside)
+        value = gated[j, TOK - STRIP:, :]
+        inside = jnp.concatenate(
+            [pick(dot(modal[j * STRIPS + a], gated[j, a * STRIP:a * STRIP + TOK, :]), STRIP) for a in range(STRIPS)], axis=0
+        )
         partial[j] = inside + skip[:, j * LANES:(j + 1) * LANES] * value.astype(f32)
 
     pltpu.make_async_copy(recv, recv, p1_recv).wait()
@@ -278,7 +311,7 @@
     pltpu.make_async_copy(prefix.at[pl.ds(cx, 1)], states.at[med_block, pl.ds(med_mode, 1)], p2_recv.at[med_block]).start()
     lax.fori_loop(1, CTX, return_one, 0)
 
-    diagonal = iota((LANES, LANES), 0) // MODES == iota((LANES, LANES), 1) // CH
+    diagonal = (iota((LANES, LANES), 0) >> 4) == (iota((LANES, LANES), 1) >> 4)
     for j in range(NB):
         pltpu.make_async_copy(states.at[j], states.at[j], p2_recv.at[j]).wait()
         spread = jnp.where(diagonal, jnp.concatenate([states[j]] * GB, axis=0), 0.0).astype(bf16)
@@ -313,17 +346,17 @@
             pltpu.VMEM((TOK, WIDE), bf16),
             pltpu.VMEM((TOK, WIDE), bf16),
             pltpu.VMEM((TOK, WIDE), bf16),
-            pltpu.VMEM((NB, 2 * TOK, LANES), bf16),
-            pltpu.VMEM((2, GROUPS, TOK // 2), bf16),
-            pltpu.VMEM((4, GROUPS, 4), bf16),
-            pltpu.VMEM((4, GROUPS, 4), bf16),
-            pltpu.VMEM((GROUPS, 2 * TOK), f32),
+            pltpu.VMEM((NB, 3 * TOK, LANES), bf16),
+            pltpu.VMEM((2, TOK // 2, PAIR), bf16),
+            pltpu.VMEM((4, 4, PAIR), bf16),
+            pltpu.VMEM((4, 4, PAIR), bf16),
+            pltpu.VMEM((PAIR, 2 * TOK), f32),
             pltpu.VMEM((GROUPS, TOK), f32),
-            pltpu.VMEM((GROUPS, TOK, 2 * TOK), bf16),
-            pltpu.VMEM((GROUPS, TOK, TOK), bf16),
+            pltpu.VMEM((NB * STRIPS, GB * STRIP, 2 * TOK), bf16),
+            pltpu.VMEM((NB * STRIPS, GB * STRIP, TOK), bf16),
             pltpu.VMEM((GROUPS * MODES, TOK), bf16),
             pltpu.VMEM((TOK, GROUPS * MODES), bf16),
-            pltpu.VMEM((NB, TOK, LANES), bf16),
+            pltpu.VMEM((NB, 2 * TOK - STRIP, LANES), bf16),
             pltpu.VMEM((NB, TOK, LANES), f32),
             pltpu.VMEM((NB, MODES, LANES), f32),
             pltpu.VMEM((CTX, LANES), f32),
@@ -333,9 +366,9 @@
             dma, dma, dma, dma((NB,)),
         ],
         compiler_params=pltpu.CompilerParams(
-            collective_id=1, has_side_effects=True, vmem_limit_bytes=48 * 1024 * 1024
+            collective_id=1, has_side_effects=True, vmem_limit_bytes=67_043_328
         ),
-    )(query, key, value, starts.reshape(CTX, TOK), taps, rate, residue, skip.reshape(1, WIDE))
+    )(query, key, value, starts.reshape(CTX, TOK), taps.T, rate.T, residue.T, skip.reshape(1, WIDE))
 
 
 def solution(mesh):

time: 59.2 us -> 48.3 us (0.82)
  the two profiles are of different devices: /device:TPU:2 before, /device:TPU:8 now
where the time goes in v2:
time: 48.3 us; the launch traced here: 48.1 us
  Pallas kernels  46.4 us (96%)
  local copies, waits for them, and re-layouts  1.67 us (3%)
    pallas_call x1, Pallas kernels, body(): pl.pallas_call(kernel, out_shape=jax.ShapeDtypeStruct((1, TOK, WIDE), bf1...  46.4 us
    unnamed x1, local copies, waits for them, and re-layouts  1.67 us

profile of v2, /device:TPU:8, one launch (start us, length us, event | category | flops | bytes accessed | tf_op | source)
XLA Modules:
  0.0 48.1 jit_solution(18440750353304718715)
XLA Ops:
  0.0 46.4 %shard_map.82 = bf16[1,128,1024]{2,1,0:T(8,128)(2,1)} custom-call(bf16[1,128,1024]{2,1,0:T(8,128)(2,1)} %q_hbm.1, bf16[1,128,1024]{2,1,0:T(8,128)(2,1)} %k_hbm.1, bf16[1,128,1024]{2,1,0:T(8,128)(2,1)} %v_hbm.1, s32[64,128]{1,0:T(8,128)} %bitcast.6, bf16[64,512]{1,0:T(8,128)(2,1)} %bitcast.5, bf16[4,256]{1,0:T(4,128)(2,1)} %bitcast.8, ...), custom_call_target="tpu_custom_call" | custom-call | tf_op jit(solution)/shard_map/pallas_call | solution.py:340
  46.4 1.7 %copy.10 = bf16[1,128,1024]{2,1,0:T(8,128)(2,1)} copy(bf16[1,128,1024]{2,1,0:T(8,128)(2,1)} %shard_map.82) | data formatting | bytes 524288

commit v3 on v2

--- a/solution.py
+++ b/solution.py
@@ -18,6 +18,7 @@
 GROUPS = WIDE // CH
 PAIR = 2 * GROUPS
 CTX = 64
+ROW = 16
 STRIP = 16
 STRIPS = TOK // STRIP
 
@@ -53,7 +54,7 @@
 def kernel(
     q_hbm, k_hbm, v_hbm, starts, taps_hbm, rate_hbm, residue_hbm, skip, out,
     q_buf, k_buf, v_buf, window, tapbuf, ratebuf, resbuf, line, hline, toep, modal, ends, carry,
-    gated, partial, e_buf, recv, prefix, states,
+    gated, partial, e_buf, recv, prefix, states, decay, no_start,
     in_sem, halo_send, halo_recv, tap_send, tap_recv, mod_send, mod_recv, p1_send, p1_recv, p2_send, p2_recv,
 ):
     fs = lax.axis_index("fsdp")
@@ -68,20 +69,30 @@
     for load in loads:
         load.start()
 
+    is_mediator = lax.rem(cx, ROW) == 0
+    med_block = cx // ROW
+
     barrier = pltpu.get_barrier_semaphore()
 
-    def greet(d, c):
-        pl.semaphore_signal(
-            barrier, inc=1, device_id=(fs, lax.rem(cx + d, CTX), dp), device_id_type=MESH
-        )
-        return c
-
-    lax.fori_loop(1, CTX, greet, 0)
+    @pl.when(cx > 0)
+    def _():
+        pl.semaphore_signal(barrier, inc=1, device_id=(fs, cx - 1, dp), device_id_type=MESH)
+
     pl.semaphore_signal(barrier, inc=1, device_id=(1 - fs, cx, dp), device_id_type=MESH)
     for d in (1, 2, 3):
         pl.semaphore_signal(
             barrier, inc=1, device_id=(fs, cx, lax.rem(dp + d, 4)), device_id_type=MESH
         )
+
+    @pl.when(is_mediator)
+    def _():
+        def greet(d, c):
+            pl.semaphore_signal(
+                barrier, inc=1, device_id=(fs, lax.rem(cx + d, CTX), dp), device_id_type=MESH
+            )
+            return c
+
+        lax.fori_loop(1, CTX, greet, 0)
 
     own_row = starts[pl.ds(cx, 1), :].astype(f32)
     before_row = starts[pl.ds(lax.rem(cx + CTX - 1, CTX), 1), :].astype(f32)
@@ -111,12 +122,12 @@
         for j in range(NB):
             window[j, :TOK, :] = jnp.zeros((TOK, LANES), bf16)
 
-    pl.semaphore_wait(barrier, CTX - 1 + 4)
+    pl.semaphore_wait(barrier, NB + 4 - jnp.where(is_mediator, 1, 0) + jnp.where(cx < CTX - 1, 1, 0))
 
     halos = [
         pltpu.make_async_remote_copy(
             window.at[j, pl.ds(TOK, TOK)], window.at[j, pl.ds(0, TOK)], halo_send.at[j], halo_recv.at[j],
-            device_id=(fs, lax.rem(cx + 1, CTX), dp), device_id_type=MESH,
+            device_id=(fs, lax.min(cx + 1, CTX - 1), dp), device_id_type=MESH,
         )
         for j in range(NB)
     ]
@@ -233,20 +244,20 @@
     steps = (iota((TOK, 1), 0) + 1).astype(f32)
     carry[...] = (jnp.exp(-rate_row * steps) * scaled_row * continues).astype(bf16)
 
-    med_mode = lax.rem(cx, MODES)
-    med_block = cx // MODES
-    rate_mode = jnp.sum(jnp.where(iota((PAIR, MODES), 1) == med_mode, rate16, 0.0), axis=1, keepdims=True)
-    group_of = half + med_block * GB + (iota((PAIR, LANES), 1) >> 4)
-    rate_med = jnp.sum(jnp.where(group_of == iota((PAIR, LANES), 0), rate_mode, 0.0), axis=0, keepdims=True)
-    no_start = jnp.where(jnp.sum(starts[...], axis=1, keepdims=True) == 0, 1.0, 0.0)
-    a = jnp.exp(-rate_med * TOK) * no_start
-    place = iota((CTX, 1), 0)
-    scales = []
-    for step in (1, 2, 4, 8, 16, 32):
-        a = jnp.where(place >= step, a, 0.0)
-        scales.append(a)
-        a = a * pltpu.roll(a, step, 0)
-
+    @pl.when(is_mediator)
+    def _():
+        group_of = half + med_block * GB + (iota((PAIR, LANES), 1) >> 4)
+        rates = dot_rows(rate16.astype(bf16), one_hot(group_of == iota((PAIR, LANES), 0)))
+        decay[...] = jnp.exp(-rates * TOK)
+        no_start[...] = jnp.broadcast_to(
+            jnp.where(jnp.sum(starts[...], axis=1, keepdims=True) == 0, 1.0, 0.0), (CTX, LANES)
+        )
+
+    @pl.when(cx == 0)
+    def _():
+        states[...] = jnp.zeros((NB, MODES, LANES), bf16)
+
+    same_group = one_hot((iota((LANES, LANES), 0) >> 4) == (iota((LANES, LANES), 1) >> 4))
     loads[2].wait()
     lane_group = iota((1, LANES), 1) >> 4
 
@@ -267,25 +278,18 @@
         value = (q_buf[:, j * LANES:(j + 1) * LANES].astype(f32) * medium.astype(bf16).astype(f32)).astype(bf16)
         gated[j, TOK - STRIP:, :] = value
         full = dot(ends[pl.ds(j * GB * MODES, GB * MODES), :], value)
-        e_buf[j] = pick(full, MODES)
-
-        def send_one(n, c):
-            to = j * MODES + n
-
-            @pl.when(to != cx)
-            def _():
-                pltpu.make_async_remote_copy(
-                    e_buf.at[j, pl.ds(n, 1)], recv.at[pl.ds(cx, 1)], p1_send, p1_recv,
-                    device_id=(fs, to, dp), device_id_type=MESH,
-                ).start()
-
-            @pl.when(to == cx)
-            def _():
-                pltpu.make_async_copy(e_buf.at[j, pl.ds(n, 1)], recv.at[pl.ds(cx, 1)], p1_recv).start()
-
-            return c
-
-        lax.fori_loop(0, MODES, send_one, 0)
+        e_buf[j] = pick(full, MODES).astype(bf16)
+
+        @pl.when(cx != j * ROW)
+        def _():
+            pltpu.make_async_remote_copy(
+                e_buf.at[j], recv.at[cx], p1_send.at[j], p1_recv.at[med_block],
+                device_id=(fs, j * ROW, dp), device_id_type=MESH,
+            ).start()
+
+        @pl.when(cx == j * ROW)
+        def _():
+            pltpu.make_async_copy(e_buf.at[j], recv.at[cx], p1_recv.at[j]).start()
 
     for j in range(NB):
         value = gated[j, TOK - STRIP:, :]
@@ -294,27 +298,39 @@
         )
         partial[j] = inside + skip[:, j * LANES:(j + 1) * LANES] * value.astype(f32)
 
-    pltpu.make_async_copy(recv, recv, p1_recv).wait()
-    b = recv[...]
-    for step, scale in zip((1, 2, 4, 8, 16, 32), scales):
-        b = b + scale * pltpu.roll(b, step, 0)
-    prefix[...] = jnp.where(place == 0, 0.0, pltpu.roll(b, 1, 0))
-
-    def return_one(d, c):
-        to = lax.rem(cx + d, CTX)
-        pltpu.make_async_remote_copy(
-            prefix.at[pl.ds(to, 1)], states.at[med_block, pl.ds(med_mode, 1)], p2_send, p2_recv.at[med_block],
-            device_id=(fs, to, dp), device_id_type=MESH,
-        ).start()
-        return c
-
-    pltpu.make_async_copy(prefix.at[pl.ds(cx, 1)], states.at[med_block, pl.ds(med_mode, 1)], p2_recv.at[med_block]).start()
-    lax.fori_loop(1, CTX, return_one, 0)
-
-    diagonal = (iota((LANES, LANES), 0) >> 4) == (iota((LANES, LANES), 1) >> 4)
+    @pl.when(is_mediator)
+    def _():
+        def return_one(to, c):
+            @pl.when(to != cx)
+            def _():
+                pltpu.make_async_remote_copy(
+                    prefix.at[to], states.at[med_block], p2_send, p2_recv.at[med_block],
+                    device_id=(fs, to, dp), device_id_type=MESH,
+                ).start()
+
+            @pl.when(to == cx)
+            def _():
+                pltpu.make_async_copy(prefix.at[to], states.at[med_block], p2_recv.at[med_block]).start()
+
+            return c
+
+        total_state = jnp.zeros((MODES, LANES), f32)
+        for y in range(CTX // ROW):
+            row = pl.ds(y * ROW, ROW)
+            pltpu.make_async_copy(recv.at[row], recv.at[row], p1_recv.at[y]).wait()
+            for p in range(y * ROW, min((y + 1) * ROW, CTX - 1)):
+                total_state = total_state * (decay[...] * no_start[pl.ds(p, 1), :]) + recv[p].astype(f32)
+                prefix[p + 1] = total_state.astype(bf16)
+            if y + 1 < CTX // ROW:
+                return_one((y + 1) * ROW, 0)
+            lax.fori_loop(y * ROW + 1, (y + 1) * ROW, return_one, 0)
+
     for j in range(NB):
-        pltpu.make_async_copy(states.at[j], states.at[j], p2_recv.at[j]).wait()
-        spread = jnp.where(diagonal, jnp.concatenate([states[j]] * GB, axis=0), 0.0).astype(bf16)
+        @pl.when(cx > 0)
+        def _():
+            pltpu.make_async_copy(states.at[j], states.at[j], p2_recv.at[j]).wait()
+
+        spread = jnp.concatenate([states[j]] * GB, axis=0) * same_group
         carried = dot(carry[:, j * LANES:(j + 1) * LANES], spread)
         out[0, :, j * LANES:(j + 1) * LANES] = (partial[j] + carried).astype(bf16)
 
@@ -323,14 +339,18 @@
         for halo in halos:
             halo.wait_send()
 
-    for sem in (p1_send, p2_send):
-        pltpu.make_async_copy(prefix.at[pl.ds(0, 56)], prefix.at[pl.ds(0, 56)], sem).wait()
-
+    for j in range(NB):
+        @pl.when(cx != j * ROW)
+        def _():
+            pltpu.make_async_copy(e_buf.at[j], e_buf.at[j], p1_send.at[j]).wait()
+
+    @pl.when(is_mediator)
+    def _():
         def drain(i, c):
-            pltpu.make_async_copy(prefix.at[pl.ds(i, 1)], prefix.at[pl.ds(i, 1)], sem).wait()
+            pltpu.make_async_copy(prefix.at[0], prefix.at[0], p2_send).wait()
             return c
 
-        lax.fori_loop(0, 7, drain, 0)
+        lax.fori_loop(0, jnp.where(cx == 0, CTX - 1, CTX - 2), drain, 0)
 
 
 def body(query, key, value, starts, taps, rate, residue, skip):
@@ -358,12 +378,14 @@
             pltpu.VMEM((TOK, GROUPS * MODES), bf16),
             pltpu.VMEM((NB, 2 * TOK - STRIP, LANES), bf16),
             pltpu.VMEM((NB, TOK, LANES), f32),
-            pltpu.VMEM((NB, MODES, LANES), f32),
+            pltpu.VMEM((NB, MODES, LANES), bf16),
+            pltpu.VMEM((CTX, MODES, LANES), bf16),
+            pltpu.VMEM((CTX, MODES, LANES), bf16),
+            pltpu.VMEM((NB, MODES, LANES), bf16),
+            pltpu.VMEM((MODES, LANES), f32),
             pltpu.VMEM((CTX, LANES), f32),
-            pltpu.VMEM((CTX, LANES), f32),
-            pltpu.VMEM((NB, MODES, LANES), f32),
             dma((6,)), dma((NB,)), dma((NB,)), dma, dma, dma((2, 3)), dma((2, 3)),
-            dma, dma, dma, dma((NB,)),
+            dma((NB,)), dma((NB,)), dma, dma((NB,)),
         ],
         compiler_params=pltpu.CompilerParams(
             collective_id=1, has_side_effects=True, vmem_limit_bytes=67_043_328

time: 48.3 us -> 36.1 us (0.75)
  the two profiles are of different devices: /device:TPU:8 before, /device:TPU:24 now
where the time goes in v3:
time: 36.1 us; the launch traced here: 35.7 us
  Pallas kernels  34 us (94%)
  local copies, waits for them, and re-layouts  1.67 us (5%)
    pallas_call x1, Pallas kernels, body(): pl.pallas_call(kernel, out_shape=jax.ShapeDtypeStruct((1, TOK, WIDE), bf1...  34 us
    unnamed x1, local copies, waits for them, and re-layouts  1.67 us

profile of v3, /device:TPU:24, one launch (start us, length us, event | category | flops | bytes accessed | tf_op | source)
XLA Modules:
  0.0 35.7 jit_solution(2941882955381765253)
XLA Ops:
  0.0 34.0 %shard_map.82 = bf16[1,128,1024]{2,1,0:T(8,128)(2,1)} custom-call(bf16[1,128,1024]{2,1,0:T(8,128)(2,1)} %q_hbm.1, bf16[1,128,1024]{2,1,0:T(8,128)(2,1)} %k_hbm.1, bf16[1,128,1024]{2,1,0:T(8,128)(2,1)} %v_hbm.1, s32[64,128]{1,0:T(8,128)} %bitcast.6, bf16[64,512]{1,0:T(8,128)(2,1)} %bitcast.5, bf16[4,256]{1,0:T(4,128)(2,1)} %bitcast.8, ...), custom_call_target="tpu_custom_call" | custom-call | tf_op jit(solution)/shard_map/pallas_call | solution.py:360
  34.0 1.7 %copy.10 = bf16[1,128,1024]{2,1,0:T(8,128)(2,1)} copy(bf16[1,128,1024]{2,1,0:T(8,128)(2,1)} %shard_map.82) | data formatting | bytes 524288

commit v4 on v3

--- a/solution.py
+++ b/solution.py
@@ -54,7 +54,7 @@
 def kernel(
     q_hbm, k_hbm, v_hbm, starts, taps_hbm, rate_hbm, residue_hbm, skip, out,
     q_buf, k_buf, v_buf, window, tapbuf, ratebuf, resbuf, line, hline, toep, modal, ends, carry,
-    gated, partial, e_buf, recv, prefix, states, decay, no_start,
+    gated, partial, e_buf, recv, prefix, states, decay, no_start, powers_buf,
     in_sem, halo_send, halo_recv, tap_send, tap_recv, mod_send, mod_recv, p1_send, p1_recv, p2_send, p2_recv,
 ):
     fs = lax.axis_index("fsdp")
@@ -207,12 +207,45 @@
         return dot(spread.astype(bf16), ones)
 
     rate_col = column(rate16)
-    scaled_col = scaled_of(rate_col, column(res16))
     lag = ((TOK - STRIP - iota((1, TOK), 1)) & (TOK - 1)).astype(f32)
     powers = jnp.exp(-rate_col * lag)
-    hline[...] = jnp.sum((powers * scaled_col).reshape(GROUPS, MODES, TOK), axis=1)
+    powers_buf[...] = powers
     ends[...] = (pltpu.roll(powers, STRIP - 1, 1) * keep).astype(bf16)
 
+    loads[2].wait()
+    lane_group = iota((1, LANES), 1) >> 4
+
+    def pick(rows, size):
+        out_rows = rows[:size]
+        for i in range(1, GB):
+            out_rows = jnp.where(lane_group == i, rows[i * size:(i + 1) * size], out_rows)
+        return out_rows
+
+    for j in range(NB):
+        @pl.when(cx > 0)
+        def _():
+            halos[j].wait_recv()
+
+        medium = jnp.concatenate(
+            [pick(dot(toep[j * STRIPS + a], window[j, a * STRIP:a * STRIP + 2 * TOK, :]), STRIP) for a in range(STRIPS)], axis=0
+        )
+        value = (q_buf[:, j * LANES:(j + 1) * LANES].astype(f32) * medium.astype(bf16).astype(f32)).astype(bf16)
+        gated[j, TOK - STRIP:, :] = value
+        full = dot(ends[pl.ds(j * GB * MODES, GB * MODES), :], value)
+        e_buf[j] = pick(full, MODES).astype(bf16)
+
+        @pl.when(cx != j * ROW)
+        def _():
+            pltpu.make_async_remote_copy(
+                e_buf.at[j], recv.at[cx], p1_send.at[j], p1_recv.at[med_block],
+                device_id=(fs, j * ROW, dp), device_id_type=MESH,
+            ).start()
+
+        @pl.when(cx == j * ROW)
+        def _():
+            pltpu.make_async_copy(e_buf.at[j], recv.at[cx], p1_recv.at[j]).start()
+
+    hline[...] = jnp.sum((powers_buf[...] * scaled_of(rate_col, column(res16))).reshape(GROUPS, MODES, TOK), axis=1)
     lane = iota((STRIP, TOK), 1)
     masks = []
     for a in range(STRIPS):
@@ -258,39 +291,6 @@
         states[...] = jnp.zeros((NB, MODES, LANES), bf16)
 
     same_group = one_hot((iota((LANES, LANES), 0) >> 4) == (iota((LANES, LANES), 1) >> 4))
-    loads[2].wait()
-    lane_group = iota((1, LANES), 1) >> 4
-
-    def pick(rows, size):
-        out_rows = rows[:size]
-        for i in range(1, GB):
-            out_rows = jnp.where(lane_group == i, rows[i * size:(i + 1) * size], out_rows)
-        return out_rows
-
-    for j in range(NB):
-        @pl.when(cx > 0)
-        def _():
-            halos[j].wait_recv()
-
-        medium = jnp.concatenate(
-            [pick(dot(toep[j * STRIPS + a], window[j, a * STRIP:a * STRIP + 2 * TOK, :]), STRIP) for a in range(STRIPS)], axis=0
-        )
-        value = (q_buf[:, j * LANES:(j + 1) * LANES].astype(f32) * medium.astype(bf16).astype(f32)).astype(bf16)
-        gated[j, TOK - STRIP:, :] = value
-        full = dot(ends[pl.ds(j * GB * MODES, GB * MODES), :], value)
-        e_buf[j] = pick(full, MODES).astype(bf16)
-
-        @pl.when(cx != j * ROW)
-        def _():
-            pltpu.make_async_remote_copy(
-                e_buf.at[j], recv.at[cx], p1_send.at[j], p1_recv.at[med_block],
-                device_id=(fs, j * ROW, dp), device_id_type=MESH,
-            ).start()
-
-        @pl.when(cx == j * ROW)
-        def _():
-            pltpu.make_async_copy(e_buf.at[j], recv.at[cx], p1_recv.at[j]).start()
-
     for j in range(NB):
         value = gated[j, TOK - STRIP:, :]
         inside = jnp.concatenate(
@@ -354,12 +354,12 @@
 
 
 def body(query, key, value, starts, taps, rate, residue, skip):
-    any_space = pl.BlockSpec(memory_space=pl.ANY)
+    any_space = pl.BlockSpec(memory_space=pltpu.MemorySpace.HBM)
     vmem = pl.BlockSpec(memory_space=pltpu.VMEM)
     dma = pltpu.SemaphoreType.DMA
     return pl.pallas_call(
         kernel,
-        out_shape=jax.ShapeDtypeStruct((1, TOK, WIDE), bf16),
+        out_shape=pltpu.VMEM((1, TOK, WIDE), bf16),
         in_specs=[any_space] * 3 + [vmem] + [any_space] * 3 + [vmem],
         out_specs=vmem,
         scratch_shapes=[
@@ -384,11 +384,12 @@
             pltpu.VMEM((NB, MODES, LANES), bf16),
             pltpu.VMEM((MODES, LANES), f32),
             pltpu.VMEM((CTX, LANES), f32),
+            pltpu.VMEM((GROUPS * MODES, TOK), f32),
             dma((6,)), dma((NB,)), dma((NB,)), dma, dma, dma((2, 3)), dma((2, 3)),
             dma((NB,)), dma((NB,)), dma, dma((NB,)),
         ],
         compiler_params=pltpu.CompilerParams(
-            collective_id=1, has_side_effects=True, vmem_limit_bytes=67_043_328
+            collective_id=1, has_side_effects=True, vmem_limit_bytes=60000000
         ),
     )(query, key, value, starts.reshape(CTX, TOK), taps.T, rate.T, residue.T, skip.reshape(1, WIDE))
 

time: 36.1 us -> 33.2 us (0.920)
  the two profiles are of different devices: /device:TPU:24 before, /device:TPU:56 now
where the time goes in v4:
time: 33.2 us; the launch traced here: 32.9 us
  Pallas kernels  32.2 us (97%)
  local copies, waits for them, and re-layouts  0.71 us (2%)
    pallas_call x1, Pallas kernels, body(): pl.pallas_call(kernel, out_shape=pltpu.VMEM((1, TOK, WIDE), bf16), in_spe...  32.2 us
    unnamed x1, local copies, waits for them, and re-layouts  0.71 us

profile of v4, /device:TPU:56, one launch (start us, length us, event | category | flops | bytes accessed | tf_op | source)
XLA Modules:
  0.0 32.9 jit_solution(16902737625955264118)
XLA Ops:
  0.0 32.2 %shard_map.82 = bf16[1,128,1024]{2,1,0:T(8,128)(2,1)S(1)} custom-call(bf16[1,128,1024]{2,1,0:T(8,128)(2,1)} %q_hbm.1, bf16[1,128,1024]{2,1,0:T(8,128)(2,1)} %k_hbm.1, bf16[1,128,1024]{2,1,0:T(8,128)(2,1)} %v_hbm.1, s32[64,128]{1,0:T(8,128)} %bitcast.6, bf16[64,512]{1,0:T(8,128)(2,1)} %bitcast.5, bf16[4,256]{1,0:T(4,128)(2,1)} %bitcast.8, ...), custom_call_target="tpu_custom_call" | custom-call | tf_op jit(solution)/shard_map/pallas_call | solution.py:360
  32.2 0.7 %copy.10 = bf16[1,128,1024]{2,1,0:T(8,128)(2,1)} copy(bf16[1,128,1024]{2,1,0:T(8,128)(2,1)S(1)} %shard_map.82) | data formatting | bytes 524288

commit v5 on v4

--- a/solution.py
+++ b/solution.py
@@ -19,6 +19,7 @@
 PAIR = 2 * GROUPS
 CTX = 64
 ROW = 16
+SEAT = 1
 STRIP = 16
 STRIPS = TOK // STRIP
 
@@ -69,7 +70,8 @@
     for load in loads:
         load.start()
 
-    is_mediator = lax.rem(cx, ROW) == 0
+    is_mediator = lax.rem(cx, ROW) == SEAT
+    opens_row = (lax.rem(cx, ROW) == 0) & (cx > 0)
     med_block = cx // ROW
 
     barrier = pltpu.get_barrier_semaphore()
@@ -93,6 +95,13 @@
             return c
 
         lax.fori_loop(1, CTX, greet, 0)
+
+    @pl.when(opens_row)
+    def _():
+        for j in range(NB):
+            pl.semaphore_signal(
+                barrier, inc=1, device_id=(fs, j * ROW + SEAT, dp), device_id_type=MESH
+            )
 
     own_row = starts[pl.ds(cx, 1), :].astype(f32)
     before_row = starts[pl.ds(lax.rem(cx + CTX - 1, CTX), 1), :].astype(f32)
@@ -122,7 +131,7 @@
         for j in range(NB):
             window[j, :TOK, :] = jnp.zeros((TOK, LANES), bf16)
 
-    pl.semaphore_wait(barrier, NB + 4 - jnp.where(is_mediator, 1, 0) + jnp.where(cx < CTX - 1, 1, 0))
+    pl.semaphore_wait(barrier, NB + 4 + jnp.where(is_mediator, CTX // ROW - 2, 0) + jnp.where(cx < CTX - 1, 1, 0))
 
     halos = [
         pltpu.make_async_remote_copy(
@@ -185,7 +194,7 @@
             toep[(g >> 4) * STRIPS + a, at, :] = base * wide_masks[a]
         return c
 
-    lax.fori_loop(0, GROUPS, build_medium, 0, unroll=8)
+    lax.fori_loop(0, GROUPS, build_medium, 0, unroll=16)
 
     rate_own.wait()
     residue_own.wait()
@@ -234,14 +243,14 @@
         full = dot(ends[pl.ds(j * GB * MODES, GB * MODES), :], value)
         e_buf[j] = pick(full, MODES).astype(bf16)
 
-        @pl.when(cx != j * ROW)
+        @pl.when(cx != j * ROW + SEAT)
         def _():
             pltpu.make_async_remote_copy(
                 e_buf.at[j], recv.at[cx], p1_send.at[j], p1_recv.at[med_block],
-                device_id=(fs, j * ROW, dp), device_id_type=MESH,
+                device_id=(fs, j * ROW + SEAT, dp), device_id_type=MESH,
             ).start()
 
-        @pl.when(cx == j * ROW)
+        @pl.when(cx == j * ROW + SEAT)
         def _():
             pltpu.make_async_copy(e_buf.at[j], recv.at[cx], p1_recv.at[j]).start()
 
@@ -263,7 +272,7 @@
             modal[(g >> 4) * STRIPS + a, at, :] = base * masks[a]
         return c
 
-    lax.fori_loop(0, GROUPS, build_modal, 0, unroll=8)
+    lax.fori_loop(0, GROUPS, build_modal, 0, unroll=16)
 
     tile = one_hot((iota((MODES, GROUPS * MODES), 1) & 15) == iota((MODES, GROUPS * MODES), 0))
     own_group = half + (iota((PAIR, GROUPS * MODES), 1) >> 4) == iota((PAIR, GROUPS * MODES), 0)
@@ -340,7 +349,7 @@
             halo.wait_send()
 
     for j in range(NB):
-        @pl.when(cx != j * ROW)
+        @pl.when(cx != j * ROW + SEAT)
         def _():
             pltpu.make_async_copy(e_buf.at[j], e_buf.at[j], p1_send.at[j]).wait()
 
@@ -350,7 +359,7 @@
             pltpu.make_async_copy(prefix.at[0], prefix.at[0], p2_send).wait()
             return c
 
-        lax.fori_loop(0, jnp.where(cx == 0, CTX - 1, CTX - 2), drain, 0)
+        lax.fori_loop(0, CTX - 2, drain, 0)
 
 
 def body(query, key, value, starts, taps, rate, residue, skip):

time: 33.2 us -> 33.5 us (level)
  the two profiles are of different devices: /device:TPU:56 before, /device:TPU:24 now
where the time goes in v5:
time: 33.5 us; the launch traced here: 33.2 us
  Pallas kernels  32.5 us (97%)
  local copies, waits for them, and re-layouts  0.71 us (2%)
    pallas_call x1, Pallas kernels, body(): pl.pallas_call(kernel, out_shape=pltpu.VMEM((1, TOK, WIDE), bf16), in_spe...  32.5 us
    unnamed x1, local copies, waits for them, and re-layouts  0.71 us

profile of v5, /device:TPU:24, one launch (start us, length us, event | category | flops | bytes accessed | tf_op | source)
XLA Modules:
  0.0 33.2 jit_solution(3561892916199556429)
XLA Ops:
  0.0 32.5 %shard_map.82 = bf16[1,128,1024]{2,1,0:T(8,128)(2,1)S(1)} custom-call(bf16[1,128,1024]{2,1,0:T(8,128)(2,1)} %q_hbm.1, bf16[1,128,1024]{2,1,0:T(8,128)(2,1)} %k_hbm.1, bf16[1,128,1024]{2,1,0:T(8,128)(2,1)} %v_hbm.1, s32[64,128]{1,0:T(8,128)} %bitcast.6, bf16[64,512]{1,0:T(8,128)(2,1)} %bitcast.5, bf16[4,256]{1,0:T(4,128)(2,1)} %bitcast.8, ...), custom_call_target="tpu_custom_call" | custom-call | tf_op jit(solution)/shard_map/pallas_call | solution.py:369
  32.5 0.7 %copy.10 = bf16[1,128,1024]{2,1,0:T(8,128)(2,1)} copy(bf16[1,128,1024]{2,1,0:T(8,128)(2,1)S(1)} %shard_map.82) | data formatting | bytes 524288

commit v6 on v4

--- a/solution.py
+++ b/solution.py
@@ -19,6 +19,7 @@
 PAIR = 2 * GROUPS
 CTX = 64
 ROW = 16
+PART = 8
 STRIP = 16
 STRIPS = TOK // STRIP
 
@@ -71,6 +72,7 @@
 
     is_mediator = lax.rem(cx, ROW) == 0
     med_block = cx // ROW
+    part_of = cx // PART
 
     barrier = pltpu.get_barrier_semaphore()
 
@@ -124,13 +126,20 @@
 
     pl.semaphore_wait(barrier, NB + 4 - jnp.where(is_mediator, 1, 0) + jnp.where(cx < CTX - 1, 1, 0))
 
-    halos = [
-        pltpu.make_async_remote_copy(
-            window.at[j, pl.ds(TOK, TOK)], window.at[j, pl.ds(0, TOK)], halo_send.at[j], halo_recv.at[j],
-            device_id=(fs, lax.min(cx + 1, CTX - 1), dp), device_id_type=MESH,
-        )
-        for j in range(NB)
-    ]
+    def order(row):
+        return [lax.rem(row + d, NB) for d in (2, 3, 1, 0)]
+
+    def halo_copies(row):
+        return [
+            pltpu.make_async_remote_copy(
+                window.at[j, pl.ds(TOK, TOK)], window.at[j, pl.ds(0, TOK)], halo_send.at[j], halo_recv.at[j],
+                device_id=(fs, lax.rem(cx + 1, CTX), dp), device_id_type=MESH,
+            )
+            for j in order(row)
+        ]
+
+    halos = halo_copies(lax.rem(cx + 1, CTX) // ROW)
+    arriving = halo_copies(med_block)
 
     @pl.when(cx < CTX - 1)
     def _():
@@ -185,7 +194,7 @@
             toep[(g >> 4) * STRIPS + a, at, :] = base * wide_masks[a]
         return c
 
-    lax.fori_loop(0, GROUPS, build_medium, 0, unroll=8)
+    lax.fori_loop(0, GROUPS, build_medium, 0, unroll=16)
 
     rate_own.wait()
     residue_own.wait()
@@ -221,29 +230,29 @@
             out_rows = jnp.where(lane_group == i, rows[i * size:(i + 1) * size], out_rows)
         return out_rows
 
-    for j in range(NB):
+    for i, j in enumerate(order(med_block)):
         @pl.when(cx > 0)
         def _():
-            halos[j].wait_recv()
+            arriving[i].wait_recv()
 
         medium = jnp.concatenate(
             [pick(dot(toep[j * STRIPS + a], window[j, a * STRIP:a * STRIP + 2 * TOK, :]), STRIP) for a in range(STRIPS)], axis=0
         )
-        value = (q_buf[:, j * LANES:(j + 1) * LANES].astype(f32) * medium.astype(bf16).astype(f32)).astype(bf16)
+        value = (q_buf[:, pl.ds(pl.multiple_of(j * LANES, LANES), LANES)].astype(f32) * medium.astype(bf16).astype(f32)).astype(bf16)
         gated[j, TOK - STRIP:, :] = value
-        full = dot(ends[pl.ds(j * GB * MODES, GB * MODES), :], value)
+        full = dot(ends[pl.ds(pl.multiple_of(j * GB * MODES, GB * MODES), GB * MODES), :], value)
         e_buf[j] = pick(full, MODES).astype(bf16)
 
         @pl.when(cx != j * ROW)
         def _():
             pltpu.make_async_remote_copy(
-                e_buf.at[j], recv.at[cx], p1_send.at[j], p1_recv.at[med_block],
+                e_buf.at[j], recv.at[cx], p1_send.at[j], p1_recv.at[part_of],
                 device_id=(fs, j * ROW, dp), device_id_type=MESH,
             ).start()
 
         @pl.when(cx == j * ROW)
         def _():
-            pltpu.make_async_copy(e_buf.at[j], recv.at[cx], p1_recv.at[j]).start()
+            pltpu.make_async_copy(e_buf.at[j], recv.at[cx], p1_recv.at[part_of]).start()
 
     hline[...] = jnp.sum((powers_buf[...] * scaled_of(rate_col, column(res16))).reshape(GROUPS, MODES, TOK), axis=1)
     lane = iota((STRIP, TOK), 1)
@@ -263,7 +272,7 @@
             modal[(g >> 4) * STRIPS + a, at, :] = base * masks[a]
         return c
 
-    lax.fori_loop(0, GROUPS, build_modal, 0, unroll=8)
+    lax.fori_loop(0, GROUPS, build_modal, 0, unroll=16)
 
     tile = one_hot((iota((MODES, GROUPS * MODES), 1) & 15) == iota((MODES, GROUPS * MODES), 0))
     own_group = half + (iota((PAIR, GROUPS * MODES), 1) >> 4) == iota((PAIR, GROUPS * MODES), 0)
@@ -315,15 +324,17 @@
             return c
 
         total_state = jnp.zeros((MODES, LANES), f32)
-        for y in range(CTX // ROW):
-            row = pl.ds(y * ROW, ROW)
-            pltpu.make_async_copy(recv.at[row], recv.at[row], p1_recv.at[y]).wait()
-            for p in range(y * ROW, min((y + 1) * ROW, CTX - 1)):
+        for part in range(CTX // PART):
+            rows = pl.ds(part * PART, PART)
+            pltpu.make_async_copy(recv.at[rows], recv.at[rows], p1_recv.at[part]).wait()
+            last = min((part + 1) * PART, CTX - 1)
+            for p in range(part * PART, last):
                 total_state = total_state * (decay[...] * no_start[pl.ds(p, 1), :]) + recv[p].astype(f32)
                 prefix[p + 1] = total_state.astype(bf16)
-            if y + 1 < CTX // ROW:
-                return_one((y + 1) * ROW, 0)
-            lax.fori_loop(y * ROW + 1, (y + 1) * ROW, return_one, 0)
+            if last % ROW == 0:
+                return_one(last, 0)
+            opens = part * PART % ROW == 0
+            lax.fori_loop(part * PART + opens, (part + 1) * PART, return_one, 0)
 
     for j in range(NB):
         @pl.when(cx > 0)
@@ -386,7 +397,7 @@
             pltpu.VMEM((CTX, LANES), f32),
             pltpu.VMEM((GROUPS * MODES, TOK), f32),
             dma((6,)), dma((NB,)), dma((NB,)), dma, dma, dma((2, 3)), dma((2, 3)),
-            dma((NB,)), dma((NB,)), dma, dma((NB,)),
+            dma((NB,)), dma((CTX // PART,)), dma, dma((NB,)),
         ],
         compiler_params=pltpu.CompilerParams(
             collective_id=1, has_side_effects=True, vmem_limit_bytes=60000000

time: 33.2 us -> 34 us (1.024)
  Pallas kernels: 32.2 us -> 33.1 us
    pallas_call x1, Pallas kernels: 32.2 us -> 33.1 us  [body(): pl.pallas_call(kernel, out_shape=pltpu.VMEM((1, TOK, WIDE), bf16), in_spe...]
where the time goes in v6:
time: 34 us; the launch traced here: 33.8 us
  Pallas kernels  33.1 us (97%)
  local copies, waits for them, and re-layouts  0.71 us (2%)
    pallas_call x1, Pallas kernels, body(): pl.pallas_call(kernel, out_shape=pltpu.VMEM((1, TOK, WIDE), bf16), in_spe...  33.1 us
    unnamed x1, local copies, waits for them, and re-layouts  0.71 us

profile of v6, /device:TPU:56, one launch (start us, length us, event | category | flops | bytes accessed | tf_op | source)
XLA Modules:
  0.0 33.8 jit_solution(1192129244374308631)
XLA Ops:
  0.0 33.1 %shard_map.82 = bf16[1,128,1024]{2,1,0:T(8,128)(2,1)S(1)} custom-call(bf16[1,128,1024]{2,1,0:T(8,128)(2,1)} %q_hbm.1, bf16[1,128,1024]{2,1,0:T(8,128)(2,1)} %k_hbm.1, bf16[1,128,1024]{2,1,0:T(8,128)(2,1)} %v_hbm.1, s32[64,128]{1,0:T(8,128)} %bitcast.6, bf16[64,512]{1,0:T(8,128)(2,1)} %bitcast.5, bf16[4,256]{1,0:T(4,128)(2,1)} %bitcast.8, ...), custom_call_target="tpu_custom_call" | custom-call | tf_op jit(solution)/shard_map/pallas_call | solution.py:371
  33.1 0.7 %copy.10 = bf16[1,128,1024]{2,1,0:T(8,128)(2,1)} copy(bf16[1,128,1024]{2,1,0:T(8,128)(2,1)S(1)} %shard_map.82) | data formatting | bytes 524288

commit v7 on v6

--- a/solution.py
+++ b/solution.py
@@ -307,6 +307,18 @@
         )
         partial[j] = inside + skip[:, j * LANES:(j + 1) * LANES] * value.astype(f32)
 
+    def finish(waits=True):
+        for j in range(NB):
+            if waits:
+                pltpu.make_async_copy(states.at[j], states.at[j], p2_recv.at[j]).wait()
+            spread = jnp.concatenate([states[j]] * GB, axis=0) * same_group
+            carried = dot(carry[:, j * LANES:(j + 1) * LANES], spread)
+            out[0, :, j * LANES:(j + 1) * LANES] = (partial[j] + carried).astype(bf16)
+
+    @pl.when(cx == 0)
+    def _():
+        finish(waits=False)
+
     @pl.when(is_mediator)
     def _():
         def return_one(to, c):
@@ -335,15 +347,14 @@
                 return_one(last, 0)
             opens = part * PART % ROW == 0
             lax.fori_loop(part * PART + opens, (part + 1) * PART, return_one, 0)
-
-    for j in range(NB):
-        @pl.when(cx > 0)
-        def _():
-            pltpu.make_async_copy(states.at[j], states.at[j], p2_recv.at[j]).wait()
-
-        spread = jnp.concatenate([states[j]] * GB, axis=0) * same_group
-        carried = dot(carry[:, j * LANES:(j + 1) * LANES], spread)
-        out[0, :, j * LANES:(j + 1) * LANES] = (partial[j] + carried).astype(bf16)
+            if (part + 1) * PART % ROW == 0 and part * PART >= ROW:
+                @pl.when(med_block == part * PART // ROW)
+                def _():
+                    finish()
+
+    @pl.when(jnp.logical_not(is_mediator))
+    def _():
+        finish()
 
     @pl.when(cx < CTX - 1)
     def _():

time: 34 us -> 37.4 us (1.100)
  the two profiles are of different devices: /device:TPU:56 before, /device:TPU:24 now
where the time goes in v7:
time: 37.4 us; the launch traced here: 37.1 us
  Pallas kernels  36.4 us (97%)
  local copies, waits for them, and re-layouts  0.71 us (2%)
    pallas_call x1, Pallas kernels, body(): pl.pallas_call(kernel, out_shape=pltpu.VMEM((1, TOK, WIDE), bf16), in_spe...  36.4 us

profile of v7, /device:TPU:24, one launch (start us, length us, event | category | flops | bytes accessed | tf_op | source)
XLA Modules:
  0.0 37.1 jit_solution(15479159318534904978)
XLA Ops:
  0.0 36.4 %shard_map.82 = bf16[1,128,1024]{2,1,0:T(8,128)(2,1)S(1)} custom-call(bf16[1,128,1024]{2,1,0:T(8,128)(2,1)} %q_hbm.1, bf16[1,128,1024]{2,1,0:T(8,128)(2,1)} %k_hbm.1, bf16[1,128,1024]{2,1,0:T(8,128)(2,1)} %v_hbm.1, s32[64,128]{1,0:T(8,128)} %bitcast.6, bf16[64,512]{1,0:T(8,128)(2,1)} %bitcast.5, bf16[4,256]{1,0:T(4,128)(2,1)} %bitcast.8, ...), custom_call_target="tpu_custom_call" | custom-call | tf_op jit(solution)/shard_map/pallas_call | solution.py:382
  36.4 0.7 %copy.10 = bf16[1,128,1024]{2,1,0:T(8,128)(2,1)} copy(bf16[1,128,1024]{2,1,0:T(8,128)(2,1)S(1)} %shard_map.82) | data formatting | bytes 524288
